TPU v7x, 32 devices: a whole 2x2x4 slice. The times are simulated.
32 devices in a mesh: ctx: 16 (over z, x, core), tp: 2 (over y).
Axes of the slice: x: 2, y: 2, z: 4, core: 2. Of those that a mesh axis runs over, the one named last changes fastest.
Arguments:
- queries: bfloat16 [16384, 4096], P('ctx', 'tp'), may hold values from -96 to 96
- rotated_key_rows: bfloat16 [16384, 2048], P('ctx', 'tp'), may hold values from -5 to 5
- value_head_rows: bfloat16 [16384, 2048], P('ctx', 'tp'), may hold values from -5 to 5
- w_out: bfloat16 [16, 256, 3840], P('tp', 'ctx'), may hold values from -0.09375 to 0.09375
- post_gain: float32 [3840], replicated, may hold values from 0.25 to 1.75
- doc_lengths: int32 [16], replicated, may hold values from 1 to 4096, 16384 in all
Outputs:
- normed_out: bfloat16 [16384, 3840], P(('ctx', 'tp'))
All inputs are finite; a program needn't handle non-finite values.
Results may differ from a plain program's by a relative error of at most 0.0085.
Values may be sent and summed in bfloat16 or wider, within the bound.
No kernel may reach another device: no remote copies, remote signals or barrier semaphores. Data moves between devices by JAX's collectives and lax.ppermute only.
A program may use at most 192 MiB of HBM per device.

v0:
```python
import jax
import jax.numpy as jnp
from jax import lax
from jax.sharding import PartitionSpec as P

HEAD_SIZE = 256
ATTEND_WINDOW = 1024


def shifted(shard, axis, by):
    devices = lax.axis_size(axis)
    pairs = [(i, i + by) for i in range(devices) if 0 <= i + by < devices]
    return lax.ppermute(shard, axis, pairs)


def post_norm(summed, post_gain):
    mean_sq = jnp.mean(summed * summed, axis=-1, keepdims=True)
    return (summed * lax.rsqrt(mean_sq + 1e-06) * post_gain).astype(jnp.bfloat16)


def score_part(query_block, key_portion, kv_heads, scaling):
    key_block = key_portion.reshape(key_portion.shape[0], kv_heads, HEAD_SIZE)
    return (
        jnp.einsum("qhgd,khd->hgqk", query_block, key_block, preferred_element_type=jnp.float32)
        * scaling
    )


def on_device(queries, rotated_key_rows, value_head_rows, w_out, post_gain, doc_lengths):
    tok_local = queries.shape[0]
    kv_heads = rotated_key_rows.shape[1] // HEAD_SIZE
    heads_local = queries.shape[1] // HEAD_SIZE
    head_groups = heads_local // kv_heads
    scaling = HEAD_SIZE ** (-0.5)
    query_block_size = min(512, tok_local)
    key_block_size = ATTEND_WINDOW + query_block_size
    block_total = tok_local // query_block_size
    query_blocks = [
        queries[b * query_block_size : (b + 1) * query_block_size].reshape(
            query_block_size, kv_heads, head_groups, HEAD_SIZE
        )
        for b in range(block_total)
    ]
    key_parts = []
    val_parts = []
    arrived = shifted((rotated_key_rows, value_head_rows), "ctx", 1)
    key_parts.insert(0, arrived[0])
    val_parts.insert(0, arrived[1])
    halo_keys = key_parts[0]
    all_vals = jnp.concatenate(val_parts + [value_head_rows], axis=0)
    base = lax.axis_index("ctx") * tok_local
    qpos_all = base + jnp.arange(tok_local, dtype=jnp.int32)
    kpos_all = base - ATTEND_WINDOW + jnp.arange(ATTEND_WINDOW + tok_local, dtype=jnp.int32)
    doc_ends = jnp.cumsum(doc_lengths)
    qdoc_all = jnp.sum((doc_ends[None, :] <= qpos_all[:, None]).astype(jnp.int32), axis=1)
    kdoc_all = jnp.sum((doc_ends[None, :] <= kpos_all[:, None]).astype(jnp.int32), axis=1)
    outputs = []
    for block_id in range(block_total):
        lower = block_id * query_block_size
        local_lo = max(lower, ATTEND_WINDOW) - ATTEND_WINDOW
        local_hi = lower + key_block_size - ATTEND_WINDOW
        local_scores = score_part(
            query_blocks[block_id], rotated_key_rows[local_lo:local_hi], kv_heads, scaling
        )
        halo_scores = score_part(
            query_blocks[block_id], halo_keys[lower:ATTEND_WINDOW], kv_heads, scaling
        )
        scores = jnp.concatenate([halo_scores, local_scores], axis=-1)
        value_block = all_vals[lower : lower + key_block_size].reshape(
            key_block_size, kv_heads, HEAD_SIZE
        )
        qpos = qpos_all[lower : lower + query_block_size]
        kpos = kpos_all[lower : lower + key_block_size]
        qdoc = qdoc_all[lower : lower + query_block_size]
        kdoc = kdoc_all[lower : lower + key_block_size]
        allowed = (
            (kpos[None, :] >= 0)
            & (kpos[None, :] <= qpos[:, None])
            & (qpos[:, None] - kpos[None, :] < ATTEND_WINDOW)
            & (kdoc[None, :] == qdoc[:, None])
        )
        scores = jnp.where(allowed[None, None], scores, -jnp.inf)
        top = jnp.max(scores, axis=-1, keepdims=True)
        expo = jnp.exp(scores - top)
        weights = (expo / jnp.sum(expo, axis=-1, keepdims=True)).astype(jnp.bfloat16)
        result = jnp.einsum(
            "hgqk,khd->qhgd", weights, value_block, preferred_element_type=jnp.float32
        )
        outputs.append(
            result.reshape(query_block_size, heads_local * HEAD_SIZE).astype(jnp.bfloat16)
        )
    attn = jnp.concatenate(outputs, axis=0).reshape(tok_local, heads_local, HEAD_SIZE)
    partial_value = jnp.einsum(
        "thn,hnd->td",
        attn,
        lax.all_gather(w_out, "ctx", axis=1, tiled=True),
        preferred_element_type=jnp.float32,
    )
    mine = lax.psum_scatter(
        partial_value.astype(jnp.bfloat16), "tp", scatter_dimension=0, tiled=True
    ).astype(jnp.float32)
    return post_norm(mine, post_gain)


def solution(mesh):
    placed = (P("ctx", "tp"), P("ctx", "tp"), P("ctx", "tp"), P("tp", "ctx", None), P(), P())
    return jax.shard_map(
        on_device, mesh=mesh, in_specs=placed, out_specs=P(("ctx", "tp"), None), check_vma=False
    )
```

profile of v0, /device:TPU:28, one launch (start us, length us, event | category | flops | bytes accessed | tf_op | source)
XLA Modules:
  0.0 376.9 jit_solution(13983909736662050847)
XLA Ops:
  7.3 4.0 %copy.36 = bf16[1024,1024]{0,1:T(8,128)(2,1)} copy(bf16[1024,1024]{1,0:T(8,128)(2,1)} %param.7) | data formatting | bytes 4194304 | tf_op args[1]
  13.3 3.5 collective-permute-start
  18.2 2.8 reshape.281
  21.2 4.0 %fusion.26 = (bf16[512,2048]{1,0:T(8,128)(2,1)S(1)}, bf16[512,2048]{1,0:T(8,128)(2,1)}) fusion(bf16[1024,2048]{1,0:T(8,128)(2,1)} %param.6), kind=kLoop, calls=%fused_computation.50 | loop fusion | bytes 8388608 | tf_op jit(solution)/shard_map/slice | solution.py:39
  27.8 2.9 copy.74
  30.9 2.6 fusion.17
  36.1 6.4 %multiply_bitcast_fusion.3 = f32[4,2,512,512]{2,3,1,0:T(8,128)} fusion(bf16[512,4,256,1]{0,2,3,1:T(8,128)(2,1)S(1)} %bitcast.60, bf16[512,4,2,256]{0,3,2,1:T(8,128)(2,1)} %bitcast.57), kind=kOutput, calls=%fused_computation.22 | convolution fusion | flops 1075838976 | bytes 11534336 | tf_op jit(solution)/shard_map/qhgd,khd->hgqk/dot_general | solution.py:24
  42.5 8.1 %multiply_bitcast_fusion = f32[4,2,512,1024]{2,3,1,0:T(8,128)} fusion(bf16[512,4,2,256]{0,3,2,1:T(8,128)(2,1)S(1)} %bitcast.55, bf16[1024,4,256,1]{2,1,0,3:T(4,128)(2,1)S(1)} %bitcast.59), kind=kOutput, calls=%fused_computation.10 | convolution fusion | flops 2151677952 | bytes 20971520 | tf_op jit(solution)/shard_map/qhgd,khd->hgqk/dot_general | solution.py:24
  50.5 106.7 %collective-permute-done = bf16[1024,1024]{1,0:T(8,128)(2,1)} collective-permute-done((bf16[1024,1024]{1,0:T(8,128)(2,1)}, bf16[1024,1024]{1,0:T(8,128)(2,1)}, u32[]{:S(2)}, u32[]{:S(2)}) %collective-permute-start) | collective-permute-done | bytes 2097184 | tf_op jit(solution)/shard_map/ppermute | solution.py:13
  159.2 3.5 fusion.27
  162.7 4.7 %copy.34 = bf16[1536,1024]{0,1:T(8,128)(2,1)} copy(bf16[1536,1024]{1,0:T(8,128)(2,1)} %get-tuple-element.7) | data formatting | bytes 6291456 | tf_op jit(solution)/shard_map/slice | solution.py:69
  167.4 4.7 %multiply_bitcast_fusion.1 = f32[4,2,512,1024]{2,3,1,0:T(8,128)S(1)} fusion(bf16[1024,4,256,1]{0,2,3,1:T(8,128)(2,1)} %bitcast.28, bf16[512,4,2,256]{0,3,2,1:T(8,128)(2,1)} %bitcast.58), kind=kOutput, calls=%fused_computation.11 | convolution fusion | flops 2151677952 | bytes 20971520 | tf_op jit(solution)/shard_map/qhgd,khd->hgqk/dot_general | solution.py:24
  172.1 14.3 %fusion.33 = (f32[4,2,512]{2,1,0:T(2,128)S(1)}, f32[4,2,512,1536]{2,3,1,0:T(8,128)}) fusion(f32[4,2,512,512]{2,3,1,0:T(8,128)} %multiply_bitcast_fusion.3, f32[4,2,512,1024]{2,3,1,0:T(8,128)S(1)} %multiply_bitcast_fusion.1, pred[512,1536]{0,1:T(8,128)(4,1)S(1)} %copy-done.6), kind=kOutput, calls=%fused_computation.57 | output fusion | flops 25167360 | bytes 51134464 | tf_op jit(solution)/shard_map/sub | solution.py:84
  186.3 13.9 %fusion.22 = bf16[4,256,2,512]{3,1,2,0:T(8,128)(2,1)} fusion(bf16[1536,4,256,1]{0,2,3,1:T(8,128)(2,1)} %bitcast.62, f32[4,2,512,1536]{2,3,1,0:T(8,128)} %get-tuple-element.22, f32[4,2,512]{2,1,0:T(2,128)S(1)} %get-tuple-element.21), kind=kOutput, calls=%fused_computation.37 | convolution fusion | flops 3234856960 | bytes 30425088 | tf_op jit(solution)/shard_map/hgqk,khd->qhgd/dot_general | solution.py:86
  200.2 3.9 %copy.51 = bf16[512,8,256]{2,0,1:T(8,128)(2,1)} copy(bf16[512,8,256]{0,2,1:T(8,128)(2,1)} %bitcast.64) | data formatting | bytes 4194304 | tf_op jit(solution)/shard_map/convert_element_type | solution.py:90
  204.1 4.6 %copy.44 = bf16[1536,1024]{0,1:T(8,128)(2,1)} copy(bf16[1536,1024]{1,0:T(8,128)(2,1)} %get-tuple-element.8) | data formatting | bytes 6291456 | tf_op jit(solution)/shard_map/slice | solution.py:69
  210.0 4.6 %multiply_bitcast_fusion.2 = f32[4,2,512,512]{2,3,1,0:T(8,128)} fusion(bf16[512,4,256,1]{0,2,3,1:T(8,128)(2,1)S(1)} %bitcast.61, bf16[512,4,2,256]{0,3,2,1:T(8,128)(2,1)S(1)} %bitcast.56), kind=kOutput, calls=%fused_computation.21 | convolution fusion | flops 1075838976 | bytes 11534336 | tf_op jit(solution)/shard_map/qhgd,khd->hgqk/dot_general | solution.py:24
  214.7 16.7 %fusion.32 = (f32[4,2,512]{2,1,0:T(2,128)S(1)}, f32[4,2,512,1536]{2,3,1,0:T(8,128)}) fusion(f32[4,2,512,1024]{2,3,1,0:T(8,128)} %multiply_bitcast_fusion, f32[4,2,512,512]{2,3,1,0:T(8,128)} %multiply_bitcast_fusion.2, pred[512,1536]{0,1:T(8,128)(4,1)} %fusion.19), kind=kOutput, calls=%fused_computation.56 | output fusion | flops 25167360 | bytes 51134464 | tf_op jit(solution)/shard_map/sub | solution.py:84
  231.4 12.9 %fusion.21 = bf16[4,256,2,512]{3,1,2,0:T(8,128)(2,1)} fusion(bf16[1536,4,256,1]{0,2,3,1:T(8,128)(2,1)S(1)} %bitcast.63, f32[4,2,512,1536]{2,3,1,0:T(8,128)} %get-tuple-element.20, f32[4,2,512]{2,1,0:T(2,128)S(1)} %get-tuple-element.19), kind=kOutput, calls=%fused_computation.36 | convolution fusion | flops 3234856960 | bytes 30425088 | tf_op jit(solution)/shard_map/hgqk,khd->qhgd/dot_general | solution.py:86
  244.3 4.1 %copy.52 = bf16[512,8,256]{2,0,1:T(8,128)(2,1)} copy(bf16[512,8,256]{0,2,1:T(8,128)(2,1)} %bitcast.65) | data formatting | bytes 4194304 | tf_op jit(solution)/shard_map/convert_element_type | solution.py:90
  248.3 21.7 %bitcast_convert_fusion = bf16[1024,3840]{1,0:T(8,128)(2,1)} fusion(bf16[8,256,3840]{2,1,0:T(8,128)(2,1)} %all-gather.2.cloned.1.call-done, bf16[512,8,256]{2,0,1:T(8,128)(2,1)} %copy.52, bf16[512,8,256]{2,0,1:T(8,128)(2,1)S(1)} %copy-done.5), kind=kOutput, calls=%fused_computation.12 | convolution fusion | flops 16118448128 | bytes 27787264 | tf_op jit(solution)/shard_map/thn,hnd->td/dot_general | solution.py:93
  270.1 93.4 %reduce-scatter.2.cloned.1.call-done = bf16[512,3840]{1,0:T(8,128)(2,1)} async-done(((bf16[1024,3840]{1,0:T(8,128)(2,1)}), bf16[512,3840]{1,0:T(8,128)(2,1)}) %reduce-scatter.2.cloned.1.call-update) | async-done | bytes 3932176 | tf_op jit(solution)/shard_map/reduce_scatter | solution.py:99
  363.4 3.1 fusion.10
  366.7 3.3 fusion.12
  (42 shorter events, 13.2 us)
Async XLA Ops:
  6.5 11.7 %copy-start.2 = (bf16[1024,1024]{1,0:T(8,128)(2,1)S(1)}, bf16[1024,1024]{1,0:T(8,128)(2,1)}, u32[]{:S(2)}) copy-start(bf16[1024,1024]{1,0:T(8,128)(2,1)} %param.7) | copy-start | bytes 6291460
  6.5 241.8 %all-gather.2.cloned.1.call-start = ((), (), s32[]{:S(2)}) async-start(), calls=%async_computation.1 | async-start | bytes 16711680 | tf_op jit(solution)/shard_map/all_gather | solution.py:96
  7.3 356.2 %reduce-scatter.2.cloned.1.call-start = ((), (), s32[]{:S(2)}) async-start(), calls=%async_computation.2 | async-start | bytes 11796480 | tf_op jit(solution)/shard_map/reduce_scatter | solution.py:99
  11.3 9.7 %copy-start.8 = (s32[16]{0:T(128)S(1)}, s32[16]{0:T(128)}, u32[]{:S(2)}) copy-start(s32[16]{0:T(128)} %param.11) | copy-start | bytes 196
  11.3 156.1 %collective-permute-start.1 = (bf16[1024,1024]{0,1:T(8,128)(2,1)}, bf16[1024,1024]{0,1:T(8,128)(2,1)}, u32[]{:S(2)}, u32[]{:S(2)}) collective-permute-start(bf16[1024,1024]{0,1:T(8,128)(2,1)} %copy.36), channel_id=1, source_target_pairs={{0,2},{2,4},{4,6},{6,8},{8,10},{10,12},{12,14},{14,16},{16,18},{18... | collective-permute-start | bytes 6291464 | tf_op jit(solution)/shard_map/ppermute | solution.py:13
  13.3 143.9 %collective-permute-start = (bf16[1024,1024]{1,0:T(8,128)(2,1)}, bf16[1024,1024]{1,0:T(8,128)(2,1)}, u32[]{:S(2)}, u32[]{:S(2)}) collective-permute-start(bf16[1024,1024]{1,0:T(8,128)(2,1)} %param.8), channel_id=1, source_target_pairs={{0,2},{2,4},{4,6},{6,8},{8,10},{10,12},{12,14},{14,16},{16,18},{18... | collective-permute-start | bytes 6291464 | tf_op jit(solution)/shard_map/ppermute | solution.py:13
  36.1 6.4 %copy-start.1 = (bf16[1024,4,256]{2,1,0:T(4,128)(2,1)S(1)}, bf16[1024,4,256]{2,1,0:T(4,128)(2,1)}, u32[]{:S(2)}) copy-start(bf16[1024,4,256]{2,1,0:T(4,128)(2,1)} %reshape.281) | copy-start | bytes 6291460
  50.5 108.5 %copy-start.4 = (bf16[1024,1024]{1,0:T(8,128)(2,1)S(1)}, bf16[1024,1024]{1,0:T(8,128)(2,1)}, u32[]{:S(2)}) copy-start(bf16[1024,1024]{1,0:T(8,128)(2,1)} %param.8) | copy-start | bytes 6291460
  167.4 4.7 %copy-start.6 = (pred[512,1536]{0,1:T(8,128)(4,1)S(1)}, pred[512,1536]{0,1:T(8,128)(4,1)}, u32[]{:S(2)}) copy-start(pred[512,1536]{0,1:T(8,128)(4,1)} %fusion.17) | copy-start | bytes 2359300
  214.7 16.7 %copy-start.3 = (bf16[1536,1024]{0,1:T(8,128)(2,1)S(1)}, bf16[1536,1024]{0,1:T(8,128)(2,1)}, u32[]{:S(2)}) copy-start(bf16[1536,1024]{0,1:T(8,128)(2,1)} %copy.44) | copy-start | bytes 9437188
  244.3 4.1 %copy-start.5 = (bf16[512,8,256]{2,0,1:T(8,128)(2,1)S(1)}, bf16[512,8,256]{2,0,1:T(8,128)(2,1)}, u32[]{:S(2)}) copy-start(bf16[512,8,256]{2,0,1:T(8,128)(2,1)} %copy.51) | copy-start | bytes 6291460
  270.1 96.5 %copy-start.7 = (f32[3840]{0:T(1024)S(1)}, f32[3840]{0:T(1024)}, u32[]{:S(2)}) copy-start(f32[3840]{0:T(1024)} %param.10) | copy-start | bytes 46084
  363.4 3.3 copy-start
Sparse Core Ops, SparseCore 0:
  9.6 145.2 all-gather.1
  270.2 93.1 reduce-scatter.1
where the time goes:
time: 380 us; the launch traced here: 377 us
  waiting for transfers between devices  201 us (53%)
  matrix products  72.2 us (19%)
  other arithmetic  42.9 us (11%)
  local copies, waits for them, and re-layouts  41.8 us (11%)
  between operations  13.6 us (4%)
  starting transfers between devices  5.59 us (1%)
    ppermute x2, waiting for transfers between devices, shifted(): return lax.ppermute(shard, axis, pairs)  107 us
    reduce_scatter x1, waiting for transfers between devices, on_device(): lax.psum_scatter(partial_value.astype(jnp.bfloat16), 'tp', scatter_dimens...  93.4 us
    sub x2, other arithmetic, on_device(): expo = jnp.exp(scores - top)  30.9 us
    dot_general x2, matrix products, on_device(): jnp.einsum('hgqk,khd->qhgd', weights, value_block, preferred_element_type...  26.8 us
    dot_general x4, matrix products, score_part(): jnp.einsum('qhgd,khd->hgqk', query_block, key_block, preferred_element_ty...  23.7 us
    dot_general x1, matrix products, on_device(): jnp.einsum('thn,hnd->td', attn, lax.all_gather(w_out, 'ctx', axis=1, tile...  21.7 us
    slice x3, local copies, waits for them, and re-layouts, on_device(): all_vals[lower:lower + key_block_size]  12.8 us
    unnamed x22, local copies, waits for them, and re-layouts  11.3 us
  transfers between devices with their start and end apart: 4, of which 2 were waited for; matrix products, arithmetic and copies ran while one was open for 34% of the time, Pallas kernels for 0%

commit v1 on v0

v1 whole, which is shorter than its diff:
```python
import functools

import jax
import jax.numpy as jnp
from jax import lax
from jax.experimental import pallas as pl
from jax.experimental.pallas import tpu as pltpu
from jax.sharding import PartitionSpec as P

HEAD_SIZE = 256
ATTEND_WINDOW = 1024
MASKED = -1e30
LOG2E = 1.4426950408889634
EXP_SCALE = LOG2E * HEAD_SIZE ** (-0.5)
VMEM_BYTES = 56 << 20


def params(**kwargs):
    return pltpu.CompilerParams(vmem_limit_bytes=VMEM_BYTES, **kwargs)


def stacked_queries(q_ref, row, rows, groups):
    return jnp.concatenate(
        [q_ref[row : row + rows, h * HEAD_SIZE : (h + 1) * HEAD_SIZE] for h in range(groups)], axis=0
    )


def dot_nt(a, b):
    return lax.dot_general(a, b, (((1,), (1,)), ((), ())), preferred_element_type=jnp.float32)


def own_kernel(rows, groups, lo_ref, q_ref, k_ref, v_ref, acc_ref, stat_ref):
    tokens = q_ref.shape[0]
    for row in range(0, tokens, rows):
        keys = row + rows
        q = stacked_queries(q_ref, row, rows, groups)
        s = dot_nt(q, k_ref[:keys, :])
        lo = lo_ref[row : row + rows, :1]
        kpos = lax.broadcasted_iota(jnp.int32, (rows, keys), 1)
        qpos = row + lax.broadcasted_iota(jnp.int32, (rows, keys), 0)
        allowed = (kpos >= lo) & (kpos <= qpos)
        lane = lax.broadcasted_iota(jnp.int32, (rows, 128), 1)
        stats = jnp.zeros((rows, 128), jnp.float32)
        for h in range(groups):
            sh = jnp.where(allowed, s[h * rows : (h + 1) * rows], MASKED)
            top = jnp.max(sh, axis=1, keepdims=True)
            p = jnp.exp2((sh - top) * EXP_SCALE)
            total = jnp.sum(p, axis=1, keepdims=True)
            acc_ref[row : row + rows, h * HEAD_SIZE : (h + 1) * HEAD_SIZE] = jnp.dot(
                p.astype(jnp.bfloat16), v_ref[:keys, :], preferred_element_type=jnp.float32
            )
            stats = jnp.where(lane == 2 * h, top, stats)
            stats = jnp.where(lane == 2 * h + 1, total, stats)
        stat_ref[row : row + rows, :] = stats


def halo_kernel(rows, groups, lo_ref, q_ref, k_ref, v_ref, acc_ref, stat_ref, out_ref):
    tokens = q_ref.shape[0]
    for row in range(0, tokens, rows):
        keys = ATTEND_WINDOW - row
        q = stacked_queries(q_ref, row, rows, groups)
        s = dot_nt(q, k_ref[row:, :])
        lo = lo_ref[row : row + rows, :1]
        kpos = row - ATTEND_WINDOW + lax.broadcasted_iota(jnp.int32, (rows, keys), 1)
        allowed = kpos >= lo
        for h in range(groups):
            cols = slice(h * HEAD_SIZE, (h + 1) * HEAD_SIZE)
            sh = jnp.where(allowed, s[h * rows : (h + 1) * rows], MASKED)
            top_own = stat_ref[row : row + rows, 2 * h : 2 * h + 1]
            total_own = stat_ref[row : row + rows, 2 * h + 1 : 2 * h + 2]
            top = jnp.maximum(jnp.max(sh, axis=1, keepdims=True), top_own)
            p = jnp.exp2((sh - top) * EXP_SCALE)
            fade = jnp.exp2((top_own - top) * EXP_SCALE)
            total = jnp.sum(p, axis=1, keepdims=True) + fade * total_own
            acc = acc_ref[row : row + rows, cols] * fade + jnp.dot(
                p.astype(jnp.bfloat16), v_ref[row:, :], preferred_element_type=jnp.float32
            )
            out_ref[row : row + rows, cols] = (acc / total).astype(jnp.bfloat16)


def attention_calls(tokens, heads, kv_heads):
    groups = heads // kv_heads
    rows = min(256, tokens)
    width = groups * HEAD_SIZE
    lo_spec = pl.BlockSpec((tokens, 128), lambda g: (0, 0))
    q_spec = pl.BlockSpec((tokens, width), lambda g: (0, g))
    kv_spec = pl.BlockSpec((tokens, HEAD_SIZE), lambda g: (0, g))
    stat_spec = pl.BlockSpec((tokens, 128), lambda g: (0, g))
    flops = 2 * heads * tokens * (tokens + rows) * HEAD_SIZE
    cost = pl.CostEstimate(
        flops=4 * flops, transcendentals=heads * tokens * tokens // 2, bytes_accessed=tokens * heads * HEAD_SIZE * 8
    )
    own = pl.pallas_call(
        functools.partial(own_kernel, rows, groups),
        grid=(kv_heads,),
        in_specs=[lo_spec, q_spec, kv_spec, kv_spec],
        out_specs=[q_spec, stat_spec],
        out_shape=[
            jax.ShapeDtypeStruct((tokens, heads * HEAD_SIZE), jnp.float32),
            jax.ShapeDtypeStruct((tokens, kv_heads * 128), jnp.float32),
        ],
        compiler_params=params(),
        cost_estimate=cost,
        name="attend_own",
    )
    halo = pl.pallas_call(
        functools.partial(halo_kernel, rows, groups),
        grid=(kv_heads,),
        in_specs=[lo_spec, q_spec, kv_spec, kv_spec, q_spec, stat_spec],
        out_specs=q_spec,
        out_shape=jax.ShapeDtypeStruct((tokens, heads * HEAD_SIZE), jnp.bfloat16),
        compiler_params=params(),
        cost_estimate=cost,
        name="attend_halo",
    )
    return own, halo


def project_kernel(pieces, piece_rows, rows, where_ref, attn_ref, *refs):
    piece_refs = refs[: len(pieces)]
    out_ref, attn_buf, w_buf, sem = refs[len(pieces) :]
    start = pl.multiple_of(where_ref[sum(pieces)], rows)
    copies = [pltpu.make_async_copy(attn_ref.at[pl.ds(start, rows), :], attn_buf, sem.at[0])]
    slot = 0
    for ref, count in zip(piece_refs, pieces):
        for i in range(count):
            at = pl.multiple_of(where_ref[slot] * piece_rows, piece_rows)
            copies.append(
                pltpu.make_async_copy(ref.at[i], w_buf.at[:, pl.ds(at, piece_rows), :], sem.at[slot + 1])
            )
            slot += 1
    for copy in copies:
        copy.start()
    for copy in copies:
        copy.wait()
    depth = w_buf.shape[0] * w_buf.shape[1]
    out_ref[...] = jnp.dot(
        attn_buf[...], w_buf[...].reshape(depth, w_buf.shape[2]), preferred_element_type=jnp.float32
    ).astype(jnp.bfloat16)


def project(where, attn, piece_arrays, rows, name):
    pieces = [a.shape[0] for a in piece_arrays]
    _, heads, piece_rows, columns = piece_arrays[0].shape
    depth = attn.shape[1]
    any_spec = pl.BlockSpec(memory_space=pl.ANY)
    return pl.pallas_call(
        functools.partial(project_kernel, pieces, piece_rows, rows),
        grid_spec=pltpu.PrefetchScalarGridSpec(
            num_scalar_prefetch=1,
            grid=(1,),
            in_specs=[any_spec] * (1 + len(pieces)),
            out_specs=pl.BlockSpec((rows, columns), lambda i, where: (0, 0)),
            scratch_shapes=[
                pltpu.VMEM((rows, depth), jnp.bfloat16),
                pltpu.VMEM((heads, HEAD_SIZE, columns), jnp.bfloat16),
                pltpu.SemaphoreType.DMA((sum(pieces) + 1,)),
            ],
        ),
        out_shape=jax.ShapeDtypeStruct((rows, columns), jnp.bfloat16),
        compiler_params=params(),
        cost_estimate=pl.CostEstimate(
            flops=2 * rows * depth * columns,
            transcendentals=0,
            bytes_accessed=2 * (rows * depth + depth * columns + rows * columns),
        ),
        name=name,
    )(where, attn, *piece_arrays)


def norm_kernel(chunks, gain_ref, *refs):
    out_ref = refs[-1]
    sums, square, column = [], 0.0, 0
    for i in range(chunks):
        total = refs[i][...].astype(jnp.float32) + refs[chunks + i][...].astype(jnp.float32)
        square = square + jnp.sum(total * total, axis=1, keepdims=True)
        sums.append(total)
    factor = lax.rsqrt(square / out_ref.shape[1] + 1e-06)
    for total in sums:
        width = total.shape[1]
        gain = gain_ref[:, column : column + width]
        out_ref[:, column : column + width] = (total * factor * gain).astype(jnp.bfloat16)
        column += width


def sum_and_norm(kept, arrived, post_gain):
    rows = kept[0].shape[0]
    block = min(64, rows)
    total = sum(a.shape[1] for a in kept)
    specs = [pl.BlockSpec((block, a.shape[1]), lambda i: (i, 0)) for a in kept + arrived]
    return pl.pallas_call(
        functools.partial(norm_kernel, len(kept)),
        grid=(rows // block,),
        in_specs=[pl.BlockSpec((1, total), lambda i: (0, 0))] + specs,
        out_specs=pl.BlockSpec((block, total), lambda i: (i, 0)),
        out_shape=jax.ShapeDtypeStruct((rows, total), jnp.bfloat16),
        compiler_params=params(),
        cost_estimate=pl.CostEstimate(flops=8 * rows * total, transcendentals=rows, bytes_accessed=6 * rows * total),
        name="sum_and_norm",
    )(post_gain.reshape(1, total), *kept, *arrived)


def ctx_pairs(size, move):
    pairs = []
    for i in range(size):
        target = move(i // 4, (i // 2) % 2, i % 2)
        if target is not None:
            pairs.append((i, target[0] * 4 + target[1] * 2 + target[2]))
    return pairs


class Gather:
    def __init__(self, size):
        self.x = ctx_pairs(size, lambda z, x, c: (z, 1 - x, c))
        self.core = ctx_pairs(size, lambda z, x, c: (z, x, 1 - c))
        self.z1 = ctx_pairs(size, lambda z, x, c: (z ^ 1, x, c))
        self.z2 = ctx_pairs(size, lambda z, x, c: (3 - z, x, c) if z in (1, 2) else None)
        self.z3 = ctx_pairs(size, lambda z, x, c: (0 if z == 1 else 3, x, c) if z in (1, 2) else None)

    def send(self, array, pairs):
        return lax.ppermute(array, "ctx", pairs)

    def along_z(self, array, edge):
        near = self.send(array, self.z1)
        both = jnp.concatenate([array, near], axis=0)
        far = self.send(both, self.z2)
        passed = self.send(far, self.z3)
        return jnp.concatenate([both, jnp.where(edge, passed, far)], axis=0)

    def pieces(self, array, edge, x_first):
        if x_first:
            array = jnp.concatenate([array, self.send(array, self.x)], axis=0)
            array = self.along_z(array, edge)
        else:
            array = self.along_z(array, edge)
            array = jnp.concatenate([array, self.send(array, self.x)], axis=0)
        return [array, self.send(array, self.core)]

    def order(self, index, x_first):
        z, x, core = index // 4, (index // 2) % 2, index % 2
        far = jnp.where(z < 2, 2, 1)
        last = jnp.where(z < 2, 3, 0)
        zs = [z, z ^ 1, far, last]
        if x_first:
            places = [zz * 4 + xx * 2 for zz in zs for xx in (x, 1 - x)]
        else:
            places = [zz * 4 + xx * 2 for xx in (x, 1 - x) for zz in zs]
        return [p + core for p in places] + [p + 1 - core for p in places]


CHUNKS = ((768, True), (768, False), (768, True), (768, False), (768, False))


def on_device(queries, rotated_key_rows, value_head_rows, w_out, post_gain, doc_lengths):
    tokens = queries.shape[0]
    heads = queries.shape[1] // HEAD_SIZE
    kv_heads = rotated_key_rows.shape[1] // HEAD_SIZE
    ctx_size, tp_size = lax.axis_size("ctx"), lax.axis_size("tp")
    ctx_index, tp_index = lax.axis_index("ctx"), lax.axis_index("tp")
    grid_gather = ctx_size == 16

    forward = [(i, i + 1) for i in range(ctx_size - 1)]
    halo_keys = lax.ppermute(rotated_key_rows, "ctx", forward)
    halo_vals = lax.ppermute(value_head_rows, "ctx", forward)

    position = ctx_index * tokens + jnp.arange(tokens, dtype=jnp.int32)
    doc_ends = jnp.cumsum(doc_lengths)
    ended = doc_ends[None, :] <= position[:, None]
    doc_start = jnp.max(jnp.where(ended, doc_ends[None, :], 0), axis=1)
    low = jnp.maximum(position - (ATTEND_WINDOW - 1), doc_start) - ctx_index * tokens
    low = jnp.broadcast_to(low[:, None], (tokens, 128))

    attend_own, attend_halo = attention_calls(tokens, heads, kv_heads)
    acc, stats = attend_own(low, queries, rotated_key_rows, value_head_rows)
    attn = attend_halo(low, queries, halo_keys, halo_vals, acc, stats)

    rows = tokens // tp_size
    chunk_plan = CHUNKS if sum(c for c, _ in CHUNKS) == w_out.shape[2] else ((w_out.shape[2], False),)
    gather = Gather(ctx_size)
    kept, arrived = [], []
    column = 0
    for number, (width, x_first) in enumerate(chunk_plan):
        part = w_out[:, :, column : column + width]
        column += width
        if grid_gather:
            z = ctx_index // 4
            pieces = gather.pieces(part[None], (z == 0) | (z == 3), x_first)
            order = gather.order(ctx_index, x_first)
        else:
            pieces = [lax.all_gather(part, "ctx", axis=0, tiled=False)]
            order = list(range(ctx_size))
        order = [jnp.asarray(o, jnp.int32) for o in order]
        if tp_size == 2:
            send_at = jnp.stack(order + [((1 - tp_index) * rows).astype(jnp.int32)])
            keep_at = jnp.stack(order + [(tp_index * rows).astype(jnp.int32)])
            send = project(send_at, attn, pieces, rows, f"project_send{number}")
            arrived.append(lax.ppermute(send, "tp", [(0, 1), (1, 0)]))
            kept.append(project(keep_at, attn, pieces, rows, f"project_keep{number}"))
        else:
            all_at = jnp.stack(order + [jnp.asarray(0, jnp.int32)])
            partial = project(all_at, attn, pieces, tokens, f"project{number}")
            mine = lax.psum_scatter(partial, "tp", scatter_dimension=0, tiled=True)
            kept.append(mine)
            arrived.append(jnp.zeros_like(mine))
    return sum_and_norm(kept, arrived, post_gain)


def solution(mesh):
    placed = (P("ctx", "tp"), P("ctx", "tp"), P("ctx", "tp"), P("tp", "ctx", None), P(), P())
    return jax.shard_map(
        on_device, mesh=mesh, in_specs=placed, out_specs=P(("ctx", "tp"), None), check_vma=False
    )
```

time: 380 us -> 284 us (0.75)
  Pallas kernels: 0 us -> 114 us
  waiting for transfers between devices: 201 us -> 109 us
  matrix products: 72.2 us -> 0 us
  local copies, waits for them, and re-layouts: 41.8 us -> 7.62 us
  starting transfers between devices: 5.59 us -> 38.3 us
  other arithmetic: 42.9 us -> 10.6 us
  between operations: 13.6 us -> 0.7 us
    pallas_call x0 -> x13, Pallas kernels: none -> 114 us  [the longest x10 60 us: project(): pl.pallas_call(functools.partial(project_kernel, pieces, piece_rows, rows...]
    reduce_scatter x1 -> x0, waiting for transfers between devices: 93.4 us -> none  [on_device(): lax.psum_scatter(partial_value.astype(jnp.bfloat16), 'tp', scatter_dimens...]
    dot_general x7 -> x0, matrix products: 72.2 us -> none  [the longest x2 26.8 us: on_device(): jnp.einsum('hgqk,khd->qhgd', weights, value_block, preferred_element_type...]
    ppermute x2 -> x32, starting transfers between devices: 5.55 us -> 38.3 us  [the longest x25 29.4 us: send(): return lax.ppermute(array, 'ctx', pairs)]
    sub x2 -> x1, other arithmetic: 30.9 us -> 0.01 us  [on_device(): jnp.maximum(position - (ATTEND_WINDOW - 1), doc_start) - ctx_index * tokens]
    slice x8 -> x0, local copies, waits for them, and re-layouts: 19.5 us -> none  [the longest x3 12.8 us: on_device(): all_vals[lower:lower + key_block_size]]
    unnamed x22 -> x72, local copies, waits for them, and re-layouts: 11.3 us -> 1.94 us
    convert_element_type x2 -> x0, local copies, waits for them, and re-layouts: 7.98 us -> none  [on_device(): result.reshape(query_block_size, heads_local * HEAD_SIZE)]
  transfers between devices with their start and end apart: 4 -> 32, of which waited for: 2 -> 12; matrix products, arithmetic and copies ran while one was open for 34% -> 5% of each run, Pallas kernels for 0% -> 38%
where the time goes in v1:
time: 284 us; the launch traced here: 281 us
  Pallas kernels  114 us (40%)
  waiting for transfers between devices  109 us (38%)
  starting transfers between devices  38.3 us (13%)
  other arithmetic  10.6 us (4%)
  local copies, waits for them, and re-layouts  7.62 us (3%)
    ppermute x25, waiting for transfers between devices, send(): return lax.ppermute(array, 'ctx', pairs)  83 us
    pallas_call x10, Pallas kernels, project(): pl.pallas_call(functools.partial(project_kernel, pieces, piece_rows, rows...  60 us
    pallas_call x1, Pallas kernels, on_device(): attn = attend_halo(low, queries, halo_keys, halo_vals, acc, stats)  30.8 us
    ppermute x25, starting transfers between devices, send(): return lax.ppermute(array, 'ctx', pairs)  29.4 us
    ppermute x5, waiting for transfers between devices, on_device(): arrived.append(lax.ppermute(send, 'tp', [(0, 1), (1, 0)]))  26.2 us
    pallas_call x1, Pallas kernels, on_device(): acc, stats = attend_own(low, queries, rotated_key_rows, value_head_rows)  14.9 us
    pallas_call x1, Pallas kernels, sum_and_norm(): pl.pallas_call(functools.partial(norm_kernel, len(kept)), grid=(rows // b...  8.55 us
  transfers between devices with their start and end apart: 32, of which 12 were waited for; matrix products, arithmetic and copies ran while one was open for 5% of the time, Pallas kernels for 38%

profile of v1, /device:TPU:28, one launch (start us, length us, event | category | flops | bytes accessed | tf_op | source)
XLA Modules:
  0.0 280.7 jit_solution(13433216151303857244)
XLA Ops:
  6.0 3.3 %collective-permute-done.22 = bf16[1,8,16,768]{3,2,1,0:T(8,128)(2,1)S(1)} collective-permute-done((bf16[1,8,16,768]{3,2,1,0:T(8,128)(2,1)S(1)}, bf16[1,8,16,768]{3,2,1,0:T(8,128)(2,1)S(1)}, u32[]{:S(2)}, u32[]{:S(2)}) %collective-permute-start.22) | collective-permute-done | bytes 196640 | tf_op jit(solution)/shard_map/ppermute | solution.py:221
  23.1 5.0 %collective-permute-done.13 = bf16[2,8,16,768]{3,2,1,0:T(8,128)(2,1)S(1)} collective-permute-done((bf16[2,8,16,768]{3,2,1,0:T(8,128)(2,1)}, bf16[2,8,16,768]{3,2,1,0:T(8,128)(2,1)S(1)}, u32[]{:S(2)}, u32[]{:S(2)}) %collective-permute-start.13) | collective-permute-done | bytes 393248 | tf_op jit(solution)/shard_map/ppermute | solution.py:221
  29.7 6.8 %collective-permute-done.3 = bf16[2,8,16,768]{3,2,1,0:T(8,128)(2,1)S(1)} collective-permute-done((bf16[2,8,16,768]{3,2,1,0:T(8,128)(2,1)}, bf16[2,8,16,768]{3,2,1,0:T(8,128)(2,1)S(1)}, u32[]{:S(2)}, u32[]{:S(2)}) %collective-permute-start.3) | collective-permute-done | bytes 393248 | tf_op jit(solution)/shard_map/ppermute | solution.py:221
  40.8 4.3 %collective-permute-done.24 = bf16[2,8,16,768]{3,2,1,0:T(8,128)(2,1)} collective-permute-done((bf16[2,8,16,768]{3,2,1,0:T(8,128)(2,1)}, bf16[2,8,16,768]{3,2,1,0:T(8,128)(2,1)}, u32[]{:S(2)}, u32[]{:S(2)}) %collective-permute-start.24) | collective-permute-done | bytes 393248 | tf_op jit(solution)/shard_map/ppermute | solution.py:221
  47.7 5.6 %collective-permute-done.19 = bf16[2,8,16,768]{3,2,1,0:T(8,128)(2,1)S(1)} collective-permute-done((bf16[2,8,16,768]{3,2,1,0:T(8,128)(2,1)}, bf16[2,8,16,768]{3,2,1,0:T(8,128)(2,1)S(1)}, u32[]{:S(2)}, u32[]{:S(2)}) %collective-permute-start.19) | collective-permute-done | bytes 393248 | tf_op jit(solution)/shard_map/ppermute | solution.py:221
  55.4 3.2 %collective-permute-done.9 = bf16[2,8,16,768]{3,2,1,0:T(8,128)(2,1)S(1)} collective-permute-done((bf16[2,8,16,768]{3,2,1,0:T(8,128)(2,1)}, bf16[2,8,16,768]{3,2,1,0:T(8,128)(2,1)S(1)}, u32[]{:S(2)}, u32[]{:S(2)}) %collective-permute-start.9) | collective-permute-done | bytes 393248 | tf_op jit(solution)/shard_map/ppermute | solution.py:221
  66.9 14.9 %attend_own.1 = (f32[1024,2048]{1,0:T(8,128)}, f32[1024,512]{1,0:T(8,128)}) custom-call(s32[1024,128]{1,0:T(8,128)} %broadcast_in_dim.35.lo_ref, bf16[1024,2048]{1,0:T(8,128)(2,1)} %q_ref.3, bf16[1024,1024]{1,0:T(8,128)(2,1)} %k_ref.1, bf16[1024,1024]{1,0:T(8,128)(2,1)} %v_ref.1), custom_call_target="tpu_custom_call" | custom-call | flops 21474836480 | bytes 16777216 | tf_op jit(solution)/shard_map/attend_own/pallas_call | solution.py:274
  83.3 38.0 %collective-permute-done.20 = bf16[4,8,16,768]{3,2,1,0:T(8,128)(2,1)S(1)} collective-permute-done((bf16[4,8,16,768]{3,2,1,0:T(8,128)(2,1)S(1)}, bf16[4,8,16,768]{3,2,1,0:T(8,128)(2,1)S(1)}, u32[]{:S(2)}, u32[]{:S(2)}) %collective-permute-start.20) | collective-permute-done | bytes 786464 | tf_op jit(solution)/shard_map/ppermute | solution.py:221
  125.3 13.0 %collective-permute-done.10 = bf16[4,8,16,768]{3,2,1,0:T(8,128)(2,1)} collective-permute-done((bf16[4,8,16,768]{3,2,1,0:T(8,128)(2,1)}, bf16[4,8,16,768]{3,2,1,0:T(8,128)(2,1)}, u32[]{:S(2)}, u32[]{:S(2)}) %collective-permute-start.10) | collective-permute-done | bytes 786464 | tf_op jit(solution)/shard_map/ppermute | solution.py:221
  143.1 4.0 %collective-permute-start.11 = (bf16[8,8,16,768]{3,2,1,0:T(8,128)(2,1)S(1)}, bf16[8,8,16,768]{3,2,1,0:T(8,128)(2,1)}, u32[]{:S(2)}, u32[]{:S(2)}) collective-permute-start(bf16[8,8,16,768]{3,2,1,0:T(8,128)(2,1)S(1)} %pad_maximum_fusion.1.refs_0_), channel_id=1, source_target_pairs={{0,2},{2,0},{4,6},{6,4},{8,10},{10,8},{12,14},{14,12},{16,18},{18,... | collective-permute-start | bytes 4718600 | tf_op jit(solution)/shard_map/ppermute | solution.py:221
  148.0 30.8 %attend_halo.1.attn_ref = bf16[1024,2048]{1,0:T(8,128)(2,1)} custom-call(s32[1024,128]{1,0:T(8,128)} %broadcast_in_dim.35.lo_ref, bf16[1024,2048]{1,0:T(8,128)(2,1)} %q_ref.3, bf16[1024,1024]{1,0:T(8,128)(2,1)} %collective-permute-done.k_ref, bf16[1024,1024]{1,0:T(8,128)(2,1)} %collective-permute-done.1.v_ref, f32[1024,2048]{1,0:T(8,128)} %get-tuple-element.7.acc_ref, ...), custom_call_target="tpu_custom_call" | custom-call | flops 21474836480 | bytes 16777216 | tf_op jit(solution)/shard_map/attend_halo/pallas_call | solution.py:275
  178.9 5.9 %project_send4.1 = bf16[512,768]{1,0:T(8,128)(2,1)} custom-call(s32[17]{0:T(128)} %stack.65.where_ref, bf16[1024,2048]{1,0:T(8,128)(2,1)} %attend_halo.1.attn_ref, bf16[8,8,16,768]{3,2,1,0:T(8,128)(2,1)} %copy-done, bf16[8,8,16,768]{3,2,1,0:T(8,128)(2,1)} %collective-permute-done.26.refs_1_), custom_call_target="tpu_custom_call" | custom-call | flops 1610612736 | bytes 6029312 | tf_op jit(solution)/shard_map/project_send4/pallas_call | solution.py:147
  185.4 6.0 %project_send3.1 = bf16[512,768]{1,0:T(8,128)(2,1)} custom-call(s32[17]{0:T(128)} %stack.65.where_ref, bf16[1024,2048]{1,0:T(8,128)(2,1)} %attend_halo.1.attn_ref, bf16[8,8,16,768]{3,2,1,0:T(8,128)(2,1)} %copy-done.1, bf16[8,8,16,768]{3,2,1,0:T(8,128)(2,1)} %collective-permute-done.21.refs_1_), custom_call_target="tpu_custom_call" | custom-call | flops 1610612736 | bytes 6029312 | tf_op jit(solution)/shard_map/project_send3/pallas_call | solution.py:147
  193.0 5.9 %project_send1.1 = bf16[512,768]{1,0:T(8,128)(2,1)} custom-call(s32[17]{0:T(128)} %stack.65.where_ref, bf16[1024,2048]{1,0:T(8,128)(2,1)} %attend_halo.1.attn_ref, bf16[8,8,16,768]{3,2,1,0:T(8,128)(2,1)} %copy-done.2, bf16[8,8,16,768]{3,2,1,0:T(8,128)(2,1)} %collective-permute-done.11.refs_1_), custom_call_target="tpu_custom_call" | custom-call | flops 1610612736 | bytes 6029312 | tf_op jit(solution)/shard_map/project_send1/pallas_call | solution.py:147
  199.5 5.9 %project_send2.1 = bf16[512,768]{1,0:T(8,128)(2,1)} custom-call(s32[17]{0:T(128)} %stack.64.where_ref, bf16[1024,2048]{1,0:T(8,128)(2,1)} %attend_halo.1.attn_ref, bf16[8,8,16,768]{3,2,1,0:T(8,128)(2,1)} %copy-done.3, bf16[8,8,16,768]{3,2,1,0:T(8,128)(2,1)} %collective-permute-done.16.refs_1_), custom_call_target="tpu_custom_call" | custom-call | flops 1610612736 | bytes 6029312 | tf_op jit(solution)/shard_map/project_send2/pallas_call | solution.py:147
  207.0 5.9 %project_send0.1 = bf16[512,768]{1,0:T(8,128)(2,1)} custom-call(s32[17]{0:T(128)} %stack.64.where_ref, bf16[1024,2048]{1,0:T(8,128)(2,1)} %attend_halo.1.attn_ref, bf16[8,8,16,768]{3,2,1,0:T(8,128)(2,1)} %copy-done.4, bf16[8,8,16,768]{3,2,1,0:T(8,128)(2,1)} %collective-permute-done.6.refs_1_), custom_call_target="tpu_custom_call" | custom-call | flops 1610612736 | bytes 6029312 | tf_op jit(solution)/shard_map/project_send0/pallas_call | solution.py:147
  215.6 6.0 %project_keep4.1.refs_4_ = bf16[512,768]{1,0:T(8,128)(2,1)} custom-call(s32[17]{0:T(128)} %stack.62.where_ref, bf16[1024,2048]{1,0:T(8,128)(2,1)} %attend_halo.1.attn_ref, bf16[8,8,16,768]{3,2,1,0:T(8,128)(2,1)} %copy-done, bf16[8,8,16,768]{3,2,1,0:T(8,128)(2,1)} %collective-permute-done.26.refs_1_), custom_call_target="tpu_custom_call" | custom-call | flops 1610612736 | bytes 6029312 | tf_op jit(solution)/shard_map/project_keep4/pallas_call | solution.py:147
  221.5 5.9 %project_keep3.1.refs_3_ = bf16[512,768]{1,0:T(8,128)(2,1)} custom-call(s32[17]{0:T(128)} %stack.62.where_ref, bf16[1024,2048]{1,0:T(8,128)(2,1)} %attend_halo.1.attn_ref, bf16[8,8,16,768]{3,2,1,0:T(8,128)(2,1)} %copy-done.1, bf16[8,8,16,768]{3,2,1,0:T(8,128)(2,1)} %collective-permute-done.21.refs_1_), custom_call_target="tpu_custom_call" | custom-call | flops 1610612736 | bytes 6029312 | tf_op jit(solution)/shard_map/project_keep3/pallas_call | solution.py:147
  227.5 6.0 %project_keep1.1.refs_1_ = bf16[512,768]{1,0:T(8,128)(2,1)} custom-call(s32[17]{0:T(128)} %stack.62.where_ref, bf16[1024,2048]{1,0:T(8,128)(2,1)} %attend_halo.1.attn_ref, bf16[8,8,16,768]{3,2,1,0:T(8,128)(2,1)} %copy-done.2, bf16[8,8,16,768]{3,2,1,0:T(8,128)(2,1)} %collective-permute-done.11.refs_1_), custom_call_target="tpu_custom_call" | custom-call | flops 1610612736 | bytes 6029312 | tf_op jit(solution)/shard_map/project_keep1/pallas_call | solution.py:147
  233.4 6.3 %project_keep2.1.refs_2_ = bf16[512,768]{1,0:T(8,128)(2,1)} custom-call(s32[17]{0:T(128)} %stack.61.where_ref, bf16[1024,2048]{1,0:T(8,128)(2,1)} %attend_halo.1.attn_ref, bf16[8,8,16,768]{3,2,1,0:T(8,128)(2,1)} %copy-done.3, bf16[8,8,16,768]{3,2,1,0:T(8,128)(2,1)} %collective-permute-done.16.refs_1_), custom_call_target="tpu_custom_call" | custom-call | flops 1610612736 | bytes 6029312 | tf_op jit(solution)/shard_map/project_keep2/pallas_call | solution.py:147
  239.8 6.1 %project_keep0.1.refs_0_ = bf16[512,768]{1,0:T(8,128)(2,1)} custom-call(s32[17]{0:T(128)} %stack.61.where_ref, bf16[1024,2048]{1,0:T(8,128)(2,1)} %attend_halo.1.attn_ref, bf16[8,8,16,768]{3,2,1,0:T(8,128)(2,1)} %copy-done.4, bf16[8,8,16,768]{3,2,1,0:T(8,128)(2,1)} %collective-permute-done.6.refs_1_), custom_call_target="tpu_custom_call" | custom-call | flops 1610612736 | bytes 6029312 | tf_op jit(solution)/shard_map/project_keep0/pallas_call | solution.py:147
  245.9 10.1 %collective-permute-done.29.refs_7_ = bf16[512,768]{1,0:T(8,128)(2,1)S(1)} collective-permute-done((bf16[512,768]{1,0:T(8,128)(2,1)}, bf16[512,768]{1,0:T(8,128)(2,1)S(1)}, u32[]{:S(2)}, u32[]{:S(2)}) %collective-permute-start.29) | collective-permute-done | bytes 786464 | tf_op jit(solution)/shard_map/ppermute | solution.py:297
  256.0 16.1 %collective-permute-done.27.refs_5_ = bf16[512,768]{1,0:T(8,128)(2,1)} collective-permute-done((bf16[512,768]{1,0:T(8,128)(2,1)}, bf16[512,768]{1,0:T(8,128)(2,1)}, u32[]{:S(2)}, u32[]{:S(2)}) %collective-permute-start.27) | collective-permute-done | bytes 786464 | tf_op jit(solution)/shard_map/ppermute | solution.py:297
  272.1 8.5 %sum_and_norm.1 = bf16[512,3840]{1,0:T(8,128)(2,1)} custom-call(f32[1,3840]{1,0:T(1,128)} %reshape.38.gain_ref, bf16[512,768]{1,0:T(8,128)(2,1)} %project_keep0.1.refs_0_, bf16[512,768]{1,0:T(8,128)(2,1)} %project_keep1.1.refs_1_, bf16[512,768]{1,0:T(8,128)(2,1)} %project_keep2.1.refs_2_, bf16[512,768]{1,0:T(8,128)(2,1)} %project_keep3.1.refs_3_, ...), custom_call_target="tpu_custom_call" | custom-call | flops 15728640 | bytes 11796480 | tf_op jit(solution)/shard_map/sum_and_norm/pallas_call | solution.py:191
  (158 shorter events, 56.3 us)
Async XLA Ops:
  13.5 24.7 %collective-permute-start.18 = (bf16[2,8,16,768]{3,2,1,0:T(8,128)(2,1)S(1)}, bf16[2,8,16,768]{3,2,1,0:T(8,128)(2,1)}, u32[]{:S(2)}, u32[]{:S(2)}) collective-permute-start(bf16[2,8,16,768]{3,2,1,0:T(8,128)(2,1)S(1)} %pad_maximum_fusion.13), channel_id=1, source_target_pairs={{8,16},{10,18},{12,20},{14,22},{16,8},{18,10},{20,12},{22,14},{9,1... | collective-permute-start | bytes 1179656 | tf_op jit(solution)/shard_map/ppermute | solution.py:221
  18.0 18.5 %collective-permute-start.3 = (bf16[2,8,16,768]{3,2,1,0:T(8,128)(2,1)}, bf16[2,8,16,768]{3,2,1,0:T(8,128)(2,1)S(1)}, u32[]{:S(2)}, u32[]{:S(2)}) collective-permute-start(bf16[2,8,16,768]{3,2,1,0:T(8,128)(2,1)} %pad_maximum_fusion.10), channel_id=1, source_target_pairs={{0,8},{2,10},{4,12},{6,14},{8,0},{10,2},{12,4},{14,6},{16,24},{18,... | collective-permute-start | bytes 1179656 | tf_op jit(solution)/shard_map/ppermute | solution.py:221
  18.7 20.8 %collective-permute-start.8 = (bf16[2,8,16,768]{3,2,1,0:T(8,128)(2,1)S(1)}, bf16[2,8,16,768]{3,2,1,0:T(8,128)(2,1)}, u32[]{:S(2)}, u32[]{:S(2)}) collective-permute-start(bf16[2,8,16,768]{3,2,1,0:T(8,128)(2,1)S(1)} %pad_maximum_fusion.11), channel_id=1, source_target_pairs={{8,16},{10,18},{12,20},{14,22},{16,8},{18,10},{20,12},{22,14},{9,1... | collective-permute-start | bytes 1179656 | tf_op jit(solution)/shard_map/ppermute | solution.py:221
  20.2 24.9 %collective-permute-start.24 = (bf16[2,8,16,768]{3,2,1,0:T(8,128)(2,1)}, bf16[2,8,16,768]{3,2,1,0:T(8,128)(2,1)}, u32[]{:S(2)}, u32[]{:S(2)}) collective-permute-start(bf16[2,8,16,768]{3,2,1,0:T(8,128)(2,1)} %collective-permute-done.23), channel_id=1, source_target_pairs={{8,0},{10,2},{12,4},{14,6},{16,24},{18,26},{20,28},{22,30},{9,1},{... | collective-permute-start | bytes 1179656 | tf_op jit(solution)/shard_map/ppermute | solution.py:221
  28.2 33.6 %collective-permute-start.14 = (bf16[4,8,16,768]{3,2,1,0:T(8,128)(2,1)S(1)}, bf16[4,8,16,768]{3,2,1,0:T(8,128)(2,1)}, u32[]{:S(2)}, u32[]{:S(2)}) collective-permute-start(bf16[4,8,16,768]{3,2,1,0:T(8,128)(2,1)S(1)} %pad_maximum_fusion.7), channel_id=1, source_target_pairs={{8,16},{10,18},{12,20},{14,22},{16,8},{18,10},{20,12},{22,14},{9,1... | collective-permute-start | bytes 2359304 | tf_op jit(solution)/shard_map/ppermute | solution.py:221
  36.6 26.8 %collective-permute-start.4 = (bf16[4,8,16,768]{3,2,1,0:T(8,128)(2,1)S(1)}, bf16[4,8,16,768]{3,2,1,0:T(8,128)(2,1)}, u32[]{:S(2)}, u32[]{:S(2)}) collective-permute-start(bf16[4,8,16,768]{3,2,1,0:T(8,128)(2,1)S(1)} %pad_maximum_fusion.5), channel_id=1, source_target_pairs={{8,16},{10,18},{12,20},{14,22},{16,8},{18,10},{20,12},{22,14},{9,1... | collective-permute-start | bytes 2359304 | tf_op jit(solution)/shard_map/ppermute | solution.py:221
  39.5 19.2 %collective-permute-start.9 = (bf16[2,8,16,768]{3,2,1,0:T(8,128)(2,1)}, bf16[2,8,16,768]{3,2,1,0:T(8,128)(2,1)S(1)}, u32[]{:S(2)}, u32[]{:S(2)}) collective-permute-start(bf16[2,8,16,768]{3,2,1,0:T(8,128)(2,1)} %collective-permute-done.8), channel_id=1, source_target_pairs={{8,0},{10,2},{12,4},{14,6},{16,24},{18,26},{20,28},{22,30},{9,1},{... | collective-permute-start | bytes 1179656 | tf_op jit(solution)/shard_map/ppermute | solution.py:221
  46.2 17.6 %collective-permute-start.25 = (bf16[4,8,16,768]{3,2,1,0:T(8,128)(2,1)S(1)}, bf16[4,8,16,768]{3,2,1,0:T(8,128)(2,1)S(1)}, u32[]{:S(2)}, u32[]{:S(2)}) collective-permute-start(bf16[4,8,16,768]{3,2,1,0:T(8,128)(2,1)S(1)} %pad_maximum_fusion.9), channel_id=1, source_target_pairs={{0,4},{2,6},{4,0},{6,2},{8,12},{10,14},{12,8},{14,10},{16,20},{18,... | collective-permute-start | bytes 2359304 | tf_op jit(solution)/shard_map/ppermute | solution.py:221
  53.3 94.0 %collective-permute-start = (bf16[1024,1024]{1,0:T(8,128)(2,1)}, bf16[1024,1024]{1,0:T(8,128)(2,1)}, u32[]{:S(2)}, u32[]{:S(2)}) collective-permute-start(bf16[1024,1024]{1,0:T(8,128)(2,1)} %k_ref.1), channel_id=1, source_target_pairs={{0,2},{2,4},{4,6},{6,8},{8,10},{10,12},{12,14},{14,16},{16,18},{18... | collective-permute-start | bytes 6291464 | tf_op jit(solution)/shard_map/ppermute | solution.py:263
  58.7 88.8 %collective-permute-start.1 = (bf16[1024,1024]{1,0:T(8,128)(2,1)}, bf16[1024,1024]{1,0:T(8,128)(2,1)}, u32[]{:S(2)}, u32[]{:S(2)}) collective-permute-start(bf16[1024,1024]{1,0:T(8,128)(2,1)} %v_ref.1), channel_id=1, source_target_pairs={{0,2},{2,4},{4,6},{6,8},{8,10},{10,12},{12,14},{14,16},{16,18},{18... | collective-permute-start | bytes 6291464 | tf_op jit(solution)/shard_map/ppermute | solution.py:264
  61.7 59.6 %collective-permute-start.20 = (bf16[4,8,16,768]{3,2,1,0:T(8,128)(2,1)S(1)}, bf16[4,8,16,768]{3,2,1,0:T(8,128)(2,1)S(1)}, u32[]{:S(2)}, u32[]{:S(2)}) collective-permute-start(bf16[4,8,16,768]{3,2,1,0:T(8,128)(2,1)S(1)} %pad_maximum_fusion.8), channel_id=1, source_target_pairs={{0,4},{2,6},{4,0},{6,2},{8,12},{10,14},{12,8},{14,10},{16,20},{18,... | collective-permute-start | bytes 2359304 | tf_op jit(solution)/shard_map/ppermute | solution.py:221
  63.4 74.8 %collective-permute-start.10 = (bf16[4,8,16,768]{3,2,1,0:T(8,128)(2,1)}, bf16[4,8,16,768]{3,2,1,0:T(8,128)(2,1)}, u32[]{:S(2)}, u32[]{:S(2)}) collective-permute-start(bf16[4,8,16,768]{3,2,1,0:T(8,128)(2,1)} %pad_maximum_fusion.6), channel_id=1, source_target_pairs={{0,4},{2,6},{4,0},{6,2},{8,12},{10,14},{12,8},{14,10},{16,20},{18,... | collective-permute-start | bytes 2359304 | tf_op jit(solution)/shard_map/ppermute | solution.py:221
  64.7 75.1 %collective-permute-start.15 = (bf16[4,8,16,768]{3,2,1,0:T(8,128)(2,1)}, bf16[4,8,16,768]{3,2,1,0:T(8,128)(2,1)}, u32[]{:S(2)}, u32[]{:S(2)}) collective-permute-start(bf16[4,8,16,768]{3,2,1,0:T(8,128)(2,1)} %collective-permute-done.14), channel_id=1, source_target_pairs={{8,0},{10,2},{12,4},{14,6},{16,24},{18,26},{20,28},{22,30},{9,1},{... | collective-permute-start | bytes 2359304 | tf_op jit(solution)/shard_map/ppermute | solution.py:221
  122.2 20.8 %collective-permute-start.5 = (bf16[4,8,16,768]{3,2,1,0:T(8,128)(2,1)}, bf16[4,8,16,768]{3,2,1,0:T(8,128)(2,1)S(1)}, u32[]{:S(2)}, u32[]{:S(2)}) collective-permute-start(bf16[4,8,16,768]{3,2,1,0:T(8,128)(2,1)} %collective-permute-done.4), channel_id=1, source_target_pairs={{8,0},{10,2},{12,4},{14,6},{16,24},{18,26},{20,28},{22,30},{9,1},{... | collective-permute-start | bytes 2359304 | tf_op jit(solution)/shard_map/ppermute | solution.py:221
  138.3 40.6 %collective-permute-start.26 = (bf16[8,8,16,768]{3,2,1,0:T(8,128)(2,1)S(1)}, bf16[8,8,16,768]{3,2,1,0:T(8,128)(2,1)}, u32[]{:S(2)}, u32[]{:S(2)}) collective-permute-start(bf16[8,8,16,768]{3,2,1,0:T(8,128)(2,1)S(1)} %pad_maximum_fusion.4.refs_0_), channel_id=1, source_target_pairs={{0,2},{2,0},{4,6},{6,4},{8,10},{10,8},{12,14},{14,12},{16,18},{18,... | collective-permute-start | bytes 4718600 | tf_op jit(solution)/shard_map/ppermute | solution.py:221
  139.7 45.6 %collective-permute-start.21 = (bf16[8,8,16,768]{3,2,1,0:T(8,128)(2,1)S(1)}, bf16[8,8,16,768]{3,2,1,0:T(8,128)(2,1)}, u32[]{:S(2)}, u32[]{:S(2)}) collective-permute-start(bf16[8,8,16,768]{3,2,1,0:T(8,128)(2,1)S(1)} %pad_maximum_fusion.3.refs_0_), channel_id=1, source_target_pairs={{0,2},{2,0},{4,6},{6,4},{8,10},{10,8},{12,14},{14,12},{16,18},{18,... | collective-permute-start | bytes 4718600 | tf_op jit(solution)/shard_map/ppermute | solution.py:221
  143.1 49.9 %collective-permute-start.11 = (bf16[8,8,16,768]{3,2,1,0:T(8,128)(2,1)S(1)}, bf16[8,8,16,768]{3,2,1,0:T(8,128)(2,1)}, u32[]{:S(2)}, u32[]{:S(2)}) collective-permute-start(bf16[8,8,16,768]{3,2,1,0:T(8,128)(2,1)S(1)} %pad_maximum_fusion.1.refs_0_), channel_id=1, source_target_pairs={{0,2},{2,0},{4,6},{6,4},{8,10},{10,8},{12,14},{14,12},{16,18},{18,... | collective-permute-start | bytes 4718600 | tf_op jit(solution)/shard_map/ppermute | solution.py:221
  147.4 52.1 %collective-permute-start.16 = (bf16[8,8,16,768]{3,2,1,0:T(8,128)(2,1)S(1)}, bf16[8,8,16,768]{3,2,1,0:T(8,128)(2,1)}, u32[]{:S(2)}, u32[]{:S(2)}) collective-permute-start(bf16[8,8,16,768]{3,2,1,0:T(8,128)(2,1)S(1)} %pad_maximum_fusion.2.refs_0_), channel_id=1, source_target_pairs={{0,2},{2,0},{4,6},{6,4},{8,10},{10,8},{12,14},{14,12},{16,18},{18,... | collective-permute-start | bytes 4718600 | tf_op jit(solution)/shard_map/ppermute | solution.py:221
  147.5 59.5 %collective-permute-start.6 = (bf16[8,8,16,768]{3,2,1,0:T(8,128)(2,1)S(1)}, bf16[8,8,16,768]{3,2,1,0:T(8,128)(2,1)}, u32[]{:S(2)}, u32[]{:S(2)}) collective-permute-start(bf16[8,8,16,768]{3,2,1,0:T(8,128)(2,1)S(1)} %pad_maximum_fusion.refs_0_), channel_id=1, source_target_pairs={{0,2},{2,0},{4,6},{6,4},{8,10},{10,8},{12,14},{14,12},{16,18},{18,... | collective-permute-start | bytes 4718600 | tf_op jit(solution)/shard_map/ppermute | solution.py:221
  184.8 61.1 %collective-permute-start.31 = (bf16[512,768]{1,0:T(8,128)(2,1)}, bf16[512,768]{1,0:T(8,128)(2,1)S(1)}, u32[]{:S(2)}, u32[]{:S(2)}) collective-permute-start(bf16[512,768]{1,0:T(8,128)(2,1)} %project_send4.1), channel_id=1, source_target_pairs={{0,1},{1,0},{2,3},{3,2},{4,5},{5,4},{6,7},{7,6},{8,9},{9,8},{10,11... | collective-permute-start | bytes 2359304 | tf_op jit(solution)/shard_map/ppermute | solution.py:297
  191.4 54.5 %collective-permute-start.30 = (bf16[512,768]{1,0:T(8,128)(2,1)}, bf16[512,768]{1,0:T(8,128)(2,1)S(1)}, u32[]{:S(2)}, u32[]{:S(2)}) collective-permute-start(bf16[512,768]{1,0:T(8,128)(2,1)} %project_send3.1), channel_id=1, source_target_pairs={{0,1},{1,0},{2,3},{3,2},{4,5},{5,4},{6,7},{7,6},{8,9},{9,8},{10,11... | collective-permute-start | bytes 2359304 | tf_op jit(solution)/shard_map/ppermute | solution.py:297
  198.9 47.0 %collective-permute-start.28 = (bf16[512,768]{1,0:T(8,128)(2,1)}, bf16[512,768]{1,0:T(8,128)(2,1)S(1)}, u32[]{:S(2)}, u32[]{:S(2)}) collective-permute-start(bf16[512,768]{1,0:T(8,128)(2,1)} %project_send1.1), channel_id=1, source_target_pairs={{0,1},{1,0},{2,3},{3,2},{4,5},{5,4},{6,7},{7,6},{8,9},{9,8},{10,11... | collective-permute-start | bytes 2359304 | tf_op jit(solution)/shard_map/ppermute | solution.py:297
  205.4 50.6 %collective-permute-start.29 = (bf16[512,768]{1,0:T(8,128)(2,1)}, bf16[512,768]{1,0:T(8,128)(2,1)S(1)}, u32[]{:S(2)}, u32[]{:S(2)}) collective-permute-start(bf16[512,768]{1,0:T(8,128)(2,1)} %project_send2.1), channel_id=1, source_target_pairs={{0,1},{1,0},{2,3},{3,2},{4,5},{5,4},{6,7},{7,6},{8,9},{9,8},{10,11... | collective-permute-start | bytes 2359304 | tf_op jit(solution)/shard_map/ppermute | solution.py:297
  213.0 59.2 %collective-permute-start.27 = (bf16[512,768]{1,0:T(8,128)(2,1)}, bf16[512,768]{1,0:T(8,128)(2,1)}, u32[]{:S(2)}, u32[]{:S(2)}) collective-permute-start(bf16[512,768]{1,0:T(8,128)(2,1)} %project_send0.1), channel_id=1, source_target_pairs={{0,1},{1,0},{2,3},{3,2},{4,5},{5,4},{6,7},{7,6},{8,9},{9,8},{10,11... | collective-permute-start | bytes 2359304 | tf_op jit(solution)/shard_map/ppermute | solution.py:297
  (44 other events, 767.2 us)

commit v2 on v0

v2 whole, which is shorter than its diff:
```python
import functools

import jax
import jax.numpy as jnp
from jax import lax
from jax.experimental import pallas as pl
from jax.experimental.pallas import tpu as pltpu
from jax.sharding import PartitionSpec as P

HEAD_SIZE = 256
ATTEND_WINDOW = 1024
MASKED = -1e30
LOG2E = 1.4426950408889634
EXP_SCALE = LOG2E * HEAD_SIZE ** (-0.5)
VMEM_BYTES = 56 << 20
BRIEF = pl.CostEstimate(flops=1, transcendentals=0, bytes_accessed=1)


def params(**kwargs):
    return pltpu.CompilerParams(vmem_limit_bytes=VMEM_BYTES, **kwargs)


def stacked_queries(q_ref, row, rows, groups):
    return jnp.concatenate(
        [q_ref[row : row + rows, h * HEAD_SIZE : (h + 1) * HEAD_SIZE] for h in range(groups)], axis=0
    )


def dot_nt(a, b):
    return lax.dot_general(a, b, (((1,), (1,)), ((), ())), preferred_element_type=jnp.float32)


def attend_kernel(rows, groups, lo_ref, q_ref, k_ref, v_ref, halo_ref, out_ref):
    tokens = q_ref.shape[0]
    for row in range(0, tokens, rows):
        q = stacked_queries(q_ref, row, rows, groups)
        lo = lo_ref[row : row + rows, :1]
        spans = [(halo_ref[row:, :HEAD_SIZE], halo_ref[row:, HEAD_SIZE:], row - ATTEND_WINDOW)]
        if row:
            spans.append((k_ref[:row, :], v_ref[:row, :], 0))
        spans.append((k_ref[row : row + rows, :], v_ref[row : row + rows, :], row))
        scores = []
        for keys, _, first in spans:
            s = dot_nt(q, keys)
            kpos = first + lax.broadcasted_iota(jnp.int32, (rows, s.shape[1]), 1)
            allowed = kpos >= lo
            if first == row:
                allowed &= kpos <= row + lax.broadcasted_iota(jnp.int32, (rows, s.shape[1]), 0)
            scores.append([jnp.where(allowed, s[h * rows : (h + 1) * rows], MASKED) for h in range(groups)])
        for h in range(groups):
            top = functools.reduce(jnp.maximum, [jnp.max(s[h], axis=1, keepdims=True) for s in scores])
            total, acc = 0.0, 0.0
            for s, (_, values, _) in zip(scores, spans):
                p = jnp.exp2((s[h] - top) * EXP_SCALE)
                total = total + jnp.sum(p, axis=1, keepdims=True)
                acc = acc + jnp.dot(p.astype(jnp.bfloat16), values, preferred_element_type=jnp.float32)
            out_ref[row : row + rows, h * HEAD_SIZE : (h + 1) * HEAD_SIZE] = (acc * (1.0 / total)).astype(jnp.bfloat16)


def attend(low, queries, keys, values, halo, head, groups):
    tokens = queries.shape[0]
    rows = min(256, tokens)
    width = groups * HEAD_SIZE
    kv_spec = pl.BlockSpec((tokens, HEAD_SIZE), lambda i: (0, head))
    return pl.pallas_call(
        functools.partial(attend_kernel, rows, groups),
        grid=(1,),
        in_specs=[
            pl.BlockSpec((tokens, 128), lambda i: (0, 0)),
            pl.BlockSpec((tokens, width), lambda i: (0, head)),
            kv_spec,
            kv_spec,
            pl.BlockSpec((tokens, 2 * HEAD_SIZE), lambda i: (0, 0)),
        ],
        out_specs=pl.BlockSpec((tokens, width), lambda i: (0, 0)),
        out_shape=jax.ShapeDtypeStruct((tokens, width), jnp.bfloat16),
        compiler_params=params(),
        cost_estimate=BRIEF,
        name=f"attend{head}",
    )(low, queries, keys, values, halo)


def project_kernel(parts, column, outs, where_ref, *refs):
    attn_refs, refs = refs[:parts], refs[parts:]
    blocks_ref, refs = refs[0], refs[1:]
    out_refs, (attn_buf, w_buf, sem, attn_sem) = refs[:outs], refs[outs:]
    blocks, heads, block_rows, _ = blocks_ref.shape
    columns = w_buf.shape[2]
    cuts = [0, columns // 256 * 128, columns]
    w_copies = []
    for half in range(2):
        span = slice(cuts[half], cuts[half + 1])
        source = slice(column + cuts[half], column + cuts[half + 1])
        copies = []
        for i in range(blocks):
            at = pl.multiple_of(where_ref[i] * block_rows, block_rows)
            copies.append(
                pltpu.make_async_copy(
                    blocks_ref.at[i, :, :, source], w_buf.at[:, pl.ds(at, block_rows), span], sem.at[half, i]
                )
            )
        w_copies.append(copies)
    width = attn_buf.shape[2] // parts
    rows = attn_buf.shape[1]
    attn_copies = []
    for out in range(outs):
        start = pl.multiple_of(where_ref[blocks + out], rows)
        attn_copies.append(
            [
                pltpu.make_async_copy(
                    ref.at[pl.ds(start, rows), :], attn_buf.at[out, :, i * width : (i + 1) * width], attn_sem.at[out, i]
                )
                for i, ref in enumerate(attn_refs)
            ]
        )
    for copy in attn_copies[0] + w_copies[0] + w_copies[1] + sum(attn_copies[1:], []):
        copy.start()
    depth = heads * HEAD_SIZE
    for out in range(outs):
        for copy in attn_copies[out]:
            copy.wait()
        for half in range(2):
            if out == 0:
                for copy in w_copies[half]:
                    copy.wait()
            span = slice(cuts[half], cuts[half + 1])
            out_refs[out][:, span] = jnp.dot(
                attn_buf[out],
                w_buf[:, :, span].reshape(depth, cuts[half + 1] - cuts[half]),
                preferred_element_type=jnp.float32,
            ).astype(jnp.bfloat16)


def project(where, attn, blocks, column, columns, outs, name):
    count, heads, _, _ = blocks.shape
    rows = attn[0].shape[0] // outs
    depth = sum(a.shape[1] for a in attn)
    any_spec = pl.BlockSpec(memory_space=pl.ANY)
    return pl.pallas_call(
        functools.partial(project_kernel, len(attn), column, outs),
        grid_spec=pltpu.PrefetchScalarGridSpec(
            num_scalar_prefetch=1,
            grid=(1,),
            in_specs=[any_spec] * (len(attn) + 1),
            out_specs=[pl.BlockSpec((rows, columns), lambda i, where: (0, 0))] * outs,
            scratch_shapes=[
                pltpu.VMEM((outs, rows, depth), jnp.bfloat16),
                pltpu.VMEM((heads, HEAD_SIZE, columns), jnp.bfloat16),
                pltpu.SemaphoreType.DMA((2, count)),
                pltpu.SemaphoreType.DMA((outs, len(attn))),
            ],
        ),
        out_shape=[jax.ShapeDtypeStruct((rows, columns), jnp.bfloat16)] * outs,
        compiler_params=params(),
        cost_estimate=BRIEF,
        name=name,
    )(where, *attn, blocks)


def norm_kernel(chunks, gain_ref, *refs):
    out_ref = refs[-1]
    sums, square, column = [], 0.0, 0
    for i in range(chunks):
        total = refs[i][...].astype(jnp.float32) + refs[chunks + i][...].astype(jnp.float32)
        square = square + jnp.sum(total * total, axis=1, keepdims=True)
        sums.append(total)
    factor = lax.rsqrt(square / out_ref.shape[1] + 1e-06)
    for total in sums:
        width = total.shape[1]
        gain = gain_ref[:, column : column + width]
        out_ref[:, column : column + width] = (total * factor * gain).astype(jnp.bfloat16)
        column += width


def sum_and_norm(kept, arrived, post_gain):
    rows = kept[0].shape[0]
    block = min(128, rows)
    total = sum(a.shape[1] for a in kept)
    specs = [pl.BlockSpec((block, a.shape[1]), lambda i: (i, 0)) for a in kept + arrived]
    return pl.pallas_call(
        functools.partial(norm_kernel, len(kept)),
        grid=(rows // block,),
        in_specs=[pl.BlockSpec((1, total), lambda i: (0, 0))] + specs,
        out_specs=pl.BlockSpec((block, total), lambda i: (i, 0)),
        out_shape=jax.ShapeDtypeStruct((rows, total), jnp.bfloat16),
        compiler_params=params(),
        cost_estimate=BRIEF,
        name="sum_and_norm",
    )(post_gain.reshape(1, total), *kept, *arrived)


def ring_order(size):
    if size % 4:
        return list(range(size))
    up = [z * 4 + core for z in range(size // 4) for core in (0, 1)]
    down = [z * 4 + 2 + core for z in reversed(range(size // 4)) for core in (0, 1)]
    return up + down


def tie(values, after):
    if after is None:
        return values
    return lax.optimization_barrier((values, after))[0]


CHUNKS = ((1024, 896), (1024, 896))


def row_limits(ctx_index, tokens, doc_lengths):
    position = ctx_index * tokens + jnp.arange(tokens, dtype=jnp.int32)
    doc_ends = jnp.cumsum(doc_lengths)
    ended = doc_ends[None, :] <= position[:, None]
    doc_start = jnp.max(jnp.where(ended, doc_ends[None, :], 0), axis=1)
    low = jnp.maximum(position - (ATTEND_WINDOW - 1), doc_start) - ctx_index * tokens
    return jnp.broadcast_to(low[:, None], (tokens, 128))


def halo_of(keys, values, head, after=None):
    size = lax.axis_size("ctx")
    cols = slice(head * HEAD_SIZE, (head + 1) * HEAD_SIZE)
    both = tie(jnp.concatenate([keys[:, cols], values[:, cols]], axis=1), after)
    return lax.ppermute(both, "ctx", [(i, i + 1) for i in range(size - 1)])


def on_device(queries, rotated_key_rows, value_head_rows, w_out, post_gain, doc_lengths):
    tokens = queries.shape[0]
    heads = queries.shape[1] // HEAD_SIZE
    kv_heads = rotated_key_rows.shape[1] // HEAD_SIZE
    ctx_size, tp_size = lax.axis_size("ctx"), lax.axis_size("tp")
    tp_index = lax.axis_index("tp")
    rows = tokens // tp_size
    low = row_limits(lax.axis_index("ctx"), tokens, doc_lengths)

    halos = []
    for head in range(kv_heads):
        cols = slice(head * HEAD_SIZE, (head + 1) * HEAD_SIZE)
        both = jnp.concatenate([rotated_key_rows[:, cols], value_head_rows[:, cols]], axis=1)
        halos.append(lax.ppermute(both, "ctx", [(i, i + 1) for i in range(ctx_size - 1)]))
    ring = ring_order(ctx_size)
    gathered, column = [], 0
    for widths in CHUNKS:
        part = w_out[:, :, column : column + sum(widths)]
        gathered.append(lax.all_gather(part, "ctx", axis=0, tiled=False, axis_index_groups=[ring]))
        column += sum(widths)

    attn = []
    for head in range(kv_heads):
        after = (halos[head], attn[-1]) if attn else halos[head]
        attn.append(
            attend(tie(low, after), queries, rotated_key_rows, value_head_rows, halos[head], head, heads // kv_heads)
        )

    kept, arrived = [], []
    for gather, widths in zip(gathered, CHUNKS):
        column = 0
        for width in widths:
            number = len(kept)
            if tp_size == 2:
                starts = jnp.stack([(1 - tp_index) * rows, tp_index * rows])
                where = jnp.concatenate([jnp.array(ring, jnp.int32), starts.astype(jnp.int32)])
                if number >= 2:
                    where = tie(where, arrived[number - 2])
                send, keep = project(where, attn, gather, column, width, 2, f"project{number}")
                arrived.append(lax.ppermute(send, "tp", [(0, 1), (1, 0)]))
            else:
                where = jnp.array(ring + [0], jnp.int32)
                (keep,) = project(where, attn, gather, column, width, 1, f"project{number}")
                if tp_size > 1:
                    keep = lax.psum_scatter(keep, "tp", scatter_dimension=0, tiled=True)
                arrived.append(jnp.zeros_like(keep))
            kept.append(keep)
            column += width
    return sum_and_norm(kept, arrived, post_gain)


def solution(mesh):
    placed = (P("ctx", "tp"), P("ctx", "tp"), P("ctx", "tp"), P("tp", "ctx", None), P(), P())
    return jax.shard_map(
        on_device, mesh=mesh, in_specs=placed, out_specs=P(("ctx", "tp"), None), check_vma=False
    )
```

time: 380 us -> 244 us (0.64)
  Pallas kernels: 0 us -> 73.7 us
  matrix products: 72.2 us -> 0 us
  waiting for transfers between devices: 201 us -> 134 us
  other arithmetic: 42.9 us -> 2.18 us
  local copies, waits for them, and re-layouts: 41.8 us -> 7.22 us
  starting transfers between devices: 5.59 us -> 12.3 us
    reduce_scatter x1 -> x0, waiting for transfers between devices: 93.4 us -> none  [on_device(): lax.psum_scatter(partial_value.astype(jnp.bfloat16), 'tp', scatter_dimens...]
    pallas_call x0 -> x9, Pallas kernels: none -> 73.7 us  [the longest x4 35.9 us: project(): pl.pallas_call(functools.partial(project_kernel, len(attn), column, outs)...]
    dot_general x7 -> x0, matrix products: 72.2 us -> none  [the longest x2 26.8 us: on_device(): jnp.einsum('hgqk,khd->qhgd', weights, value_block, preferred_element_type...]
    sub x2 -> x1, other arithmetic: 30.9 us -> 0.01 us  [row_limits(): jnp.maximum(position - (ATTEND_WINDOW - 1), doc_start) - ctx_index * tokens]
    ppermute x2 -> x8, waiting for transfers between devices: 107 us -> 134 us  [the longest x4 78.7 us: on_device(): lax.ppermute(both, 'ctx', [(i, i + 1) for i in range(ctx_size - 1)])]
    slice x8 -> x2, local copies, waits for them, and re-layouts: 19.5 us -> 4.23 us  [the longest x1 2.36 us: on_device(): part = w_out[:, :, column:column + sum(widths)]]
    unnamed x22 -> x16, local copies, waits for them, and re-layouts: 11.3 us -> 1.31 us
    convert_element_type x2 -> x0, local copies, waits for them, and re-layouts: 7.98 us -> none  [on_device(): result.reshape(query_block_size, heads_local * HEAD_SIZE)]
  transfers between devices with their start and end apart: 4 -> 10, of which waited for: 2 -> 7; matrix products, arithmetic and copies ran while one was open for 34% -> 2% of each run, Pallas kernels for 0% -> 28%
where the time goes in v2:
time: 244 us; the launch traced here: 243 us
  waiting for transfers between devices  134 us (55%)
  Pallas kernels  73.7 us (30%)
  between operations  13.6 us (6%)
  starting transfers between devices  12.3 us (5%)
  local copies, waits for them, and re-layouts  7.22 us (3%)
    ppermute x4, waiting for transfers between devices, on_device(): lax.ppermute(both, 'ctx', [(i, i + 1) for i in range(ctx_size - 1)])  78.7 us
    ppermute x4, waiting for transfers between devices, on_device(): arrived.append(lax.ppermute(send, 'tp', [(0, 1), (1, 0)]))  54.8 us
    pallas_call x4, Pallas kernels, project(): pl.pallas_call(functools.partial(project_kernel, len(attn), column, outs)...  35.9 us
    pallas_call x4, Pallas kernels, attend(): pl.pallas_call(functools.partial(attend_kernel, rows, groups), grid=(1,),...  31.2 us
    ppermute x4, starting transfers between devices, on_device(): lax.ppermute(both, 'ctx', [(i, i + 1) for i in range(ctx_size - 1)])  9.26 us
    pallas_call x1, Pallas kernels, sum_and_norm(): pl.pallas_call(functools.partial(norm_kernel, len(kept)), grid=(rows // b...  6.67 us
  transfers between devices with their start and end apart: 10, of which 7 were waited for; matrix products, arithmetic and copies ran while one was open for 2% of the time, Pallas kernels for 28%

profile of v2, /device:TPU:28, one launch (start us, length us, event | category | flops | bytes accessed | tf_op | source)
XLA Modules:
  0.0 243.2 jit_solution(1589018165706477869)
XLA Ops:
  6.5 2.4 fusion.2
  9.7 1.9 fusion
  11.7 1.9 collective-permute-start
  13.7 3.5 %collective-permute-start.1 = (bf16[1024,512]{1,0:T(8,128)(2,1)S(1)}, bf16[1024,512]{1,0:T(8,128)(2,1)}, u32[]{:S(2)}, u32[]{:S(2)}) collective-permute-start(bf16[1024,512]{1,0:T(8,128)(2,1)S(1)} %pad_maximum_fusion.1), channel_id=1, source_target_pairs={{0,2},{2,4},{4,6},{6,8},{8,10},{10,12},{12,14},{14,16},{16,18},{18... | collective-permute-start | bytes 3145736 | tf_op jit(solution)/shard_map/ppermute | solution.py:238
  17.3 1.9 collective-permute-start.2
  19.2 1.1 pad_maximum_fusion.3
  20.3 1.9 collective-permute-start.3
  23.2 25.9 %collective-permute-done.halo_ref = bf16[1024,512]{1,0:T(8,128)(2,1)} collective-permute-done((bf16[1024,512]{1,0:T(8,128)(2,1)S(1)}, bf16[1024,512]{1,0:T(8,128)(2,1)}, u32[]{:S(2)}, u32[]{:S(2)}) %collective-permute-start) | collective-permute-done | bytes 1048608 | tf_op jit(solution)/shard_map/ppermute | solution.py:238
  50.1 7.8 %attend0.1.refs_0_ = bf16[1024,512]{1,0:T(8,128)(2,1)} custom-call(s32[1024,128]{1,0:T(8,128)} %broadcast_in_dim.13.lo_ref, bf16[1024,2048]{1,0:T(8,128)(2,1)} %q_ref.7, bf16[1024,1024]{1,0:T(8,128)(2,1)} %k_ref.7, bf16[1024,1024]{1,0:T(8,128)(2,1)} %v_ref.7, bf16[1024,512]{1,0:T(8,128)(2,1)} %collective-permute-done.halo_ref), custom_call_target="tpu_custom_call" | custom-call | flops 1 | bytes 1 | tf_op jit(solution)/shard_map/attend0/pallas_call | solution.py:65
  57.8 19.1 %collective-permute-done.1.halo_ref = bf16[1024,512]{1,0:T(8,128)(2,1)} collective-permute-done((bf16[1024,512]{1,0:T(8,128)(2,1)S(1)}, bf16[1024,512]{1,0:T(8,128)(2,1)}, u32[]{:S(2)}, u32[]{:S(2)}) %collective-permute-start.1) | collective-permute-done | bytes 1048608 | tf_op jit(solution)/shard_map/ppermute | solution.py:238
  76.9 7.7 %attend1.1.refs_1_ = bf16[1024,512]{1,0:T(8,128)(2,1)} custom-call(s32[1024,128]{1,0:T(8,128)} %broadcast_in_dim.13.lo_ref, bf16[1024,2048]{1,0:T(8,128)(2,1)} %q_ref.7, bf16[1024,1024]{1,0:T(8,128)(2,1)} %k_ref.7, bf16[1024,1024]{1,0:T(8,128)(2,1)} %v_ref.7, bf16[1024,512]{1,0:T(8,128)(2,1)} %collective-permute-done.1.halo_ref), custom_call_target="tpu_custom_call" | custom-call | flops 1 | bytes 1 | tf_op jit(solution)/shard_map/attend1/pallas_call | solution.py:65
  84.6 8.0 %collective-permute-done.2.halo_ref = bf16[1024,512]{1,0:T(8,128)(2,1)} collective-permute-done((bf16[1024,512]{1,0:T(8,128)(2,1)S(1)}, bf16[1024,512]{1,0:T(8,128)(2,1)}, u32[]{:S(2)}, u32[]{:S(2)}) %collective-permute-start.2) | collective-permute-done | bytes 1048608 | tf_op jit(solution)/shard_map/ppermute | solution.py:238
  92.6 7.9 %attend2.1.refs_2_ = bf16[1024,512]{1,0:T(8,128)(2,1)} custom-call(s32[1024,128]{1,0:T(8,128)} %broadcast_in_dim.13.lo_ref, bf16[1024,2048]{1,0:T(8,128)(2,1)} %q_ref.7, bf16[1024,1024]{1,0:T(8,128)(2,1)} %k_ref.7, bf16[1024,1024]{1,0:T(8,128)(2,1)} %v_ref.7, bf16[1024,512]{1,0:T(8,128)(2,1)} %collective-permute-done.2.halo_ref), custom_call_target="tpu_custom_call" | custom-call | flops 1 | bytes 1 | tf_op jit(solution)/shard_map/attend2/pallas_call | solution.py:65
  100.5 25.8 %collective-permute-done.3.halo_ref = bf16[1024,512]{1,0:T(8,128)(2,1)} collective-permute-done((bf16[1024,512]{1,0:T(8,128)(2,1)}, bf16[1024,512]{1,0:T(8,128)(2,1)}, u32[]{:S(2)}, u32[]{:S(2)}) %collective-permute-start.3) | collective-permute-done | bytes 1048608 | tf_op jit(solution)/shard_map/ppermute | solution.py:238
  126.3 7.8 %attend3.1.refs_3_ = bf16[1024,512]{1,0:T(8,128)(2,1)} custom-call(s32[1024,128]{1,0:T(8,128)} %broadcast_in_dim.13.lo_ref, bf16[1024,2048]{1,0:T(8,128)(2,1)} %q_ref.7, bf16[1024,1024]{1,0:T(8,128)(2,1)} %k_ref.7, bf16[1024,1024]{1,0:T(8,128)(2,1)} %v_ref.7, bf16[1024,512]{1,0:T(8,128)(2,1)} %collective-permute-done.3.halo_ref), custom_call_target="tpu_custom_call" | custom-call | flops 1 | bytes 1 | tf_op jit(solution)/shard_map/attend3/pallas_call | solution.py:65
  134.1 9.1 %project0.1 = (bf16[512,1024]{1,0:T(8,128)(2,1)}, bf16[512,1024]{1,0:T(8,128)(2,1)}) custom-call(s32[18]{0:T(128)} %pad_add_fusion.where_ref, bf16[1024,512]{1,0:T(8,128)(2,1)} %attend0.1.refs_0_, bf16[1024,512]{1,0:T(8,128)(2,1)} %attend1.1.refs_1_, bf16[1024,512]{1,0:T(8,128)(2,1)} %attend2.1.refs_2_, bf16[1024,512]{1,0:T(8,128)(2,1)} %attend3.1.refs_3_, ...), custom_call_target="tpu_custom_call" | custom-call | flops 1 | bytes 1 | tf_op jit(solution)/shard_map/project0/pallas_call | solution.py:139
  143.6 9.0 %project1.1 = (bf16[512,896]{1,0:T(8,128)(2,1)}, bf16[512,896]{1,0:T(8,128)(2,1)}) custom-call(s32[18]{0:T(128)} %pad_add_fusion.where_ref, bf16[1024,512]{1,0:T(8,128)(2,1)} %attend0.1.refs_0_, bf16[1024,512]{1,0:T(8,128)(2,1)} %attend1.1.refs_1_, bf16[1024,512]{1,0:T(8,128)(2,1)} %attend2.1.refs_2_, bf16[1024,512]{1,0:T(8,128)(2,1)} %attend3.1.refs_3_, ...), custom_call_target="tpu_custom_call" | custom-call | flops 1 | bytes 1 | tf_op jit(solution)/shard_map/project1/pallas_call | solution.py:139
  152.6 1.7 collective-permute-start.5
  154.3 15.2 %collective-permute-done.4.refs_4_ = bf16[512,1024]{1,0:T(8,128)(2,1)S(1)} collective-permute-done((bf16[512,1024]{1,0:T(8,128)(2,1)}, bf16[512,1024]{1,0:T(8,128)(2,1)S(1)}, u32[]{:S(2)}, u32[]{:S(2)}) %collective-permute-start.4) | collective-permute-done | bytes 1048608 | tf_op jit(solution)/shard_map/ppermute | solution.py:264
  169.5 9.0 %project2.1 = (bf16[512,1024]{1,0:T(8,128)(2,1)}, bf16[512,1024]{1,0:T(8,128)(2,1)}) custom-call(s32[18]{0:T(128)} %pad_add_fusion.where_ref, bf16[1024,512]{1,0:T(8,128)(2,1)} %attend0.1.refs_0_, bf16[1024,512]{1,0:T(8,128)(2,1)} %attend1.1.refs_1_, bf16[1024,512]{1,0:T(8,128)(2,1)} %attend2.1.refs_2_, bf16[1024,512]{1,0:T(8,128)(2,1)} %attend3.1.refs_3_, ...), custom_call_target="tpu_custom_call" | custom-call | flops 1 | bytes 1 | tf_op jit(solution)/shard_map/project2/pallas_call | solution.py:139
  179.0 10.2 %collective-permute-done.5.refs_5_ = bf16[512,896]{1,0:T(8,128)(2,1)S(1)} collective-permute-done((bf16[512,896]{1,0:T(8,128)(2,1)}, bf16[512,896]{1,0:T(8,128)(2,1)S(1)}, u32[]{:S(2)}, u32[]{:S(2)}) %collective-permute-start.5) | collective-permute-done | bytes 917536 | tf_op jit(solution)/shard_map/ppermute | solution.py:264
  189.2 8.8 %project3.1 = (bf16[512,896]{1,0:T(8,128)(2,1)}, bf16[512,896]{1,0:T(8,128)(2,1)}) custom-call(s32[18]{0:T(128)} %pad_add_fusion.where_ref, bf16[1024,512]{1,0:T(8,128)(2,1)} %attend0.1.refs_0_, bf16[1024,512]{1,0:T(8,128)(2,1)} %attend1.1.refs_1_, bf16[1024,512]{1,0:T(8,128)(2,1)} %attend2.1.refs_2_, bf16[1024,512]{1,0:T(8,128)(2,1)} %attend3.1.refs_3_, ...), custom_call_target="tpu_custom_call" | custom-call | flops 1 | bytes 1 | tf_op jit(solution)/shard_map/project3/pallas_call | solution.py:139
  199.0 29.4 %collective-permute-done.7.refs_7_ = bf16[512,896]{1,0:T(8,128)(2,1)S(1)} collective-permute-done((bf16[512,896]{1,0:T(8,128)(2,1)}, bf16[512,896]{1,0:T(8,128)(2,1)S(1)}, u32[]{:S(2)}, u32[]{:S(2)}) %collective-permute-start.7) | collective-permute-done | bytes 917536 | tf_op jit(solution)/shard_map/ppermute | solution.py:264
  229.7 6.7 %sum_and_norm.1 = bf16[512,3840]{1,0:T(8,128)(2,1)} custom-call(f32[1,3840]{1,0:T(1,128)} %reshape.38.gain_ref, bf16[512,1024]{1,0:T(8,128)(2,1)} %get-tuple-element.23.refs_0_, bf16[512,896]{1,0:T(8,128)(2,1)} %get-tuple-element.24.refs_1_, bf16[512,1024]{1,0:T(8,128)(2,1)} %get-tuple-element.27.refs_2_, bf16[512,896]{1,0:T(8,128)(2,1)} %get-tuple-element.30.refs_3_, ...), custom_call_target="tpu_custom_call" | custom-call | flops 1 | bytes 1 | tf_op jit(solution)/shard_map/sum_and_norm/pallas_call | solution.py:180
  (38 shorter events, 6.2 us)
Async XLA Ops:
  6.5 3.1 %copy-start = (bf16[1024,1024]{1,0:T(8,128)(2,1)S(1)}, bf16[1024,1024]{1,0:T(8,128)(2,1)}, u32[]{:S(2)}) copy-start(bf16[1024,1024]{1,0:T(8,128)(2,1)} %k_ref.7) | copy-start | bytes 6291460
  6.5 127.5 %all-gather.5.cloned.1.call-start = ((), (), s32[]{:S(2)}) async-start(), calls=%async_computation | async-start | bytes 8355840 | tf_op jit(solution)/shard_map/all_gather | solution.py:243
  8.9 160.6 %all-gather.7.cloned.1.call-start = ((), (), s32[]{:S(2)}) async-start(), calls=%async_computation.1 | async-start | bytes 8355840 | tf_op jit(solution)/shard_map/all_gather | solution.py:243
  11.7 37.4 %collective-permute-start = (bf16[1024,512]{1,0:T(8,128)(2,1)S(1)}, bf16[1024,512]{1,0:T(8,128)(2,1)}, u32[]{:S(2)}, u32[]{:S(2)}) collective-permute-start(bf16[1024,512]{1,0:T(8,128)(2,1)S(1)} %pad_maximum_fusion), channel_id=1, source_target_pairs={{0,2},{2,4},{4,6},{6,8},{8,10},{10,12},{12,14},{14,16},{16,18},{18... | collective-permute-start | bytes 3145736 | tf_op jit(solution)/shard_map/ppermute | solution.py:238
  13.7 63.2 %collective-permute-start.1 = (bf16[1024,512]{1,0:T(8,128)(2,1)S(1)}, bf16[1024,512]{1,0:T(8,128)(2,1)}, u32[]{:S(2)}, u32[]{:S(2)}) collective-permute-start(bf16[1024,512]{1,0:T(8,128)(2,1)S(1)} %pad_maximum_fusion.1), channel_id=1, source_target_pairs={{0,2},{2,4},{4,6},{6,8},{8,10},{10,12},{12,14},{14,16},{16,18},{18... | collective-permute-start | bytes 3145736 | tf_op jit(solution)/shard_map/ppermute | solution.py:238
  17.2 5.0 %copy-start.6 = (s32[16]{0:T(128)S(1)}, s32[16]{0:T(128)}, u32[]{:S(2)}) copy-start(s32[16]{0:T(128)} %param.15) | copy-start | bytes 196
  17.2 5.3 %copy-start.7 = (s32[16]{0:T(128)S(1)}, s32[16]{0:T(128)}, u32[]{:S(2)}) copy-start(s32[16]{0:T(128)} %constant.26.clone) | copy-start | bytes 196
  17.3 75.3 %collective-permute-start.2 = (bf16[1024,512]{1,0:T(8,128)(2,1)S(1)}, bf16[1024,512]{1,0:T(8,128)(2,1)}, u32[]{:S(2)}, u32[]{:S(2)}) collective-permute-start(bf16[1024,512]{1,0:T(8,128)(2,1)S(1)} %pad_maximum_fusion.2), channel_id=1, source_target_pairs={{0,2},{2,4},{4,6},{6,8},{8,10},{10,12},{12,14},{14,16},{16,18},{18... | collective-permute-start | bytes 3145736 | tf_op jit(solution)/shard_map/ppermute | solution.py:238
  20.3 106.0 %collective-permute-start.3 = (bf16[1024,512]{1,0:T(8,128)(2,1)}, bf16[1024,512]{1,0:T(8,128)(2,1)}, u32[]{:S(2)}, u32[]{:S(2)}) collective-permute-start(bf16[1024,512]{1,0:T(8,128)(2,1)} %pad_maximum_fusion.3), channel_id=1, source_target_pairs={{0,2},{2,4},{4,6},{6,8},{8,10},{10,12},{12,14},{14,16},{16,18},{18... | collective-permute-start | bytes 3145736 | tf_op jit(solution)/shard_map/ppermute | solution.py:238
  143.1 26.4 %collective-permute-start.4 = (bf16[512,1024]{1,0:T(8,128)(2,1)}, bf16[512,1024]{1,0:T(8,128)(2,1)S(1)}, u32[]{:S(2)}, u32[]{:S(2)}) collective-permute-start(bf16[512,1024]{1,0:T(8,128)(2,1)} %get-tuple-element.25), channel_id=1, source_target_pairs={{0,1},{1,0},{2,3},{3,2},{4,5},{5,4},{6,7},{7,6},{8,9},{9,8},{10,11... | collective-permute-start | bytes 3145736 | tf_op jit(solution)/shard_map/ppermute | solution.py:264
  152.6 36.6 %collective-permute-start.5 = (bf16[512,896]{1,0:T(8,128)(2,1)}, bf16[512,896]{1,0:T(8,128)(2,1)S(1)}, u32[]{:S(2)}, u32[]{:S(2)}) collective-permute-start(bf16[512,896]{1,0:T(8,128)(2,1)} %get-tuple-element.28), channel_id=1, source_target_pairs={{0,1},{1,0},{2,3},{3,2},{4,5},{5,4},{6,7},{7,6},{8,9},{9,8},{10,11... | collective-permute-start | bytes 2752520 | tf_op jit(solution)/shard_map/ppermute | solution.py:264
  169.5 9.0 %copy-start.1 = (bf16[512,1024]{1,0:T(8,128)(2,1)}, bf16[512,1024]{1,0:T(8,128)(2,1)S(1)}, u32[]{:S(2)}) copy-start(bf16[512,1024]{1,0:T(8,128)(2,1)S(1)} %collective-permute-done.4.refs_4_) | copy-start | bytes 3145732
  178.5 19.9 %copy-start.5 = (f32[3840]{0:T(1024)S(1)}, f32[3840]{0:T(1024)}, u32[]{:S(2)}) copy-start(f32[3840]{0:T(1024)} %param.14) | copy-start | bytes 46084
  178.5 49.9 %collective-permute-start.6 = (bf16[512,1024]{1,0:T(8,128)(2,1)}, bf16[512,1024]{1,0:T(8,128)(2,1)S(1)}, u32[]{:S(2)}, u32[]{:S(2)}) collective-permute-start(bf16[512,1024]{1,0:T(8,128)(2,1)} %get-tuple-element.31), channel_id=1, source_target_pairs={{0,1},{1,0},{2,3},{3,2},{4,5},{5,4},{6,7},{7,6},{8,9},{9,8},{10,11... | collective-permute-start | bytes 3145736 | tf_op jit(solution)/shard_map/ppermute | solution.py:264
  189.2 8.8 %copy-start.3 = (bf16[512,896]{1,0:T(8,128)(2,1)}, bf16[512,896]{1,0:T(8,128)(2,1)S(1)}, u32[]{:S(2)}) copy-start(bf16[512,896]{1,0:T(8,128)(2,1)S(1)} %collective-permute-done.5.refs_5_) | copy-start | bytes 2752516
  198.0 30.5 %collective-permute-start.7 = (bf16[512,896]{1,0:T(8,128)(2,1)}, bf16[512,896]{1,0:T(8,128)(2,1)S(1)}, u32[]{:S(2)}, u32[]{:S(2)}) collective-permute-start(bf16[512,896]{1,0:T(8,128)(2,1)} %get-tuple-element.32), channel_id=1, source_target_pairs={{0,1},{1,0},{2,3},{3,2},{4,5},{5,4},{6,7},{7,6},{8,9},{9,8},{10,11... | collective-permute-start | bytes 2752520 | tf_op jit(solution)/shard_map/ppermute | solution.py:264
  228.4 0.9 copy-start.4
  228.4 1.3 copy-start.2
Sparse Core Ops, SparseCore 0:
  9.0 66.4 all-gather.4
  77.2 60.6 all-gather.6

commit v3 on v2

v3 whole, which is shorter than its diff:
```python
import functools

import jax
import jax.numpy as jnp
from jax import lax
from jax.experimental import pallas as pl
from jax.experimental.pallas import tpu as pltpu
from jax.sharding import PartitionSpec as P

HEAD_SIZE = 256
ATTEND_WINDOW = 1024
MASKED = -1e30
LOG2E = 1.4426950408889634
EXP_SCALE = LOG2E * HEAD_SIZE ** (-0.5)
VMEM_BYTES = 44 << 20
BRIEF = pl.CostEstimate(flops=1, transcendentals=0, bytes_accessed=1)


def params(**kwargs):
    return pltpu.CompilerParams(vmem_limit_bytes=VMEM_BYTES, **kwargs)


def stacked_queries(q_ref, row, rows, groups):
    return jnp.concatenate(
        [q_ref[row : row + rows, h * HEAD_SIZE : (h + 1) * HEAD_SIZE] for h in range(groups)], axis=0
    )


def dot_nt(a, b):
    return lax.dot_general(a, b, (((1,), (1,)), ((), ())), preferred_element_type=jnp.float32)


def attend_kernel(
    rows, groups, near_ref, lo_ref, q_hbm, k_hbm, v_hbm, chip_ref, link_ref, out_ref, q_ref, k_ref, v_ref, halo_ref, sem
):
    width = q_ref.shape[1]
    head = near_ref[1]
    key_cols = pl.ds(pl.multiple_of(head * HEAD_SIZE, HEAD_SIZE), HEAD_SIZE)
    query_cols = pl.ds(pl.multiple_of(head * width, width), width)
    copies = [
        pltpu.make_async_copy(q_hbm.at[:, query_cols], q_ref, sem.at[0]),
        pltpu.make_async_copy(k_hbm.at[:, key_cols], k_ref, sem.at[1]),
        pltpu.make_async_copy(v_hbm.at[:, key_cols], v_ref, sem.at[2]),
    ]
    for copy in copies:
        copy.start()

    @pl.when(near_ref[0] == 1)
    def _():
        pltpu.make_async_copy(chip_ref, halo_ref, sem.at[3]).start()

    @pl.when(near_ref[0] != 1)
    def _():
        pltpu.make_async_copy(link_ref, halo_ref, sem.at[3]).start()

    for copy in copies:
        copy.wait()
    pltpu.make_async_copy(chip_ref, halo_ref, sem.at[3]).wait()
    tokens = q_ref.shape[0]
    for row in range(0, tokens, rows):
        q = stacked_queries(q_ref, row, rows, groups)
        lo = lo_ref[row : row + rows, :1]
        spans = [(halo_ref[row:, :HEAD_SIZE], halo_ref[row:, HEAD_SIZE:], row - ATTEND_WINDOW)]
        if row:
            spans.append((k_ref[:row, :], v_ref[:row, :], 0))
        spans.append((k_ref[row : row + rows, :], v_ref[row : row + rows, :], row))
        scores = []
        for keys, _, first in spans:
            s = dot_nt(q, keys)
            kpos = first + lax.broadcasted_iota(jnp.int32, (rows, s.shape[1]), 1)
            allowed = kpos >= lo
            if first == row:
                allowed &= kpos <= row + lax.broadcasted_iota(jnp.int32, (rows, s.shape[1]), 0)
            scores.append([jnp.where(allowed, s[h * rows : (h + 1) * rows], MASKED) for h in range(groups)])
        for h in range(groups):
            top = functools.reduce(jnp.maximum, [jnp.max(s[h], axis=1, keepdims=True) for s in scores])
            total, acc = 0.0, 0.0
            for s, (_, values, _) in zip(scores, spans):
                p = jnp.exp2((s[h] - top) * EXP_SCALE)
                total = total + jnp.sum(p, axis=1, keepdims=True)
                acc = acc + jnp.dot(p.astype(jnp.bfloat16), values, preferred_element_type=jnp.float32)
            out_ref[row : row + rows, h * HEAD_SIZE : (h + 1) * HEAD_SIZE] = (acc * (1.0 / total)).astype(jnp.bfloat16)


def attend(near, low, queries, keys, values, halo, groups):
    tokens = queries.shape[0]
    rows = min(256, tokens)
    width = groups * HEAD_SIZE
    any_spec = pl.BlockSpec(memory_space=pl.ANY)
    vmem_spec = pl.BlockSpec(memory_space=pltpu.VMEM)
    return pl.pallas_call(
        functools.partial(attend_kernel, rows, groups),
        in_specs=[pl.BlockSpec(memory_space=pltpu.SMEM), vmem_spec] + [any_spec] * 5,
        out_specs=vmem_spec,
        scratch_shapes=[
            pltpu.VMEM((tokens, width), jnp.bfloat16),
            pltpu.VMEM((tokens, HEAD_SIZE), jnp.bfloat16),
            pltpu.VMEM((tokens, HEAD_SIZE), jnp.bfloat16),
            pltpu.VMEM((tokens, 2 * HEAD_SIZE), jnp.bfloat16),
            pltpu.SemaphoreType.DMA((4,)),
        ],
        out_shape=jax.ShapeDtypeStruct((tokens, width), jnp.bfloat16),
        compiler_params=params(),
        cost_estimate=BRIEF,
        name="attend",
    )(near, low, queries, keys, values, *halo)


def project_kernel(parts, chunk, outs, where_ref, *refs):
    attn_refs, refs = refs[:parts], refs[parts:]
    blocks_ref, refs = refs[0], refs[1:]
    out_refs, (w_buf, sem) = refs[:outs], refs[outs:]
    blocks, _, heads, block_rows, columns = blocks_ref.shape
    copies = []
    for i in range(blocks):
        at = pl.multiple_of(where_ref[i] * block_rows, block_rows)
        copies.append(
            pltpu.make_async_copy(blocks_ref.at[i, chunk], w_buf.at[:, pl.ds(at, block_rows), :], sem.at[i])
        )
    for copy in copies:
        copy.start()
    for copy in copies:
        copy.wait()
    part_heads = heads // parts
    for out in range(outs):
        rows = out_refs[out].shape[0]
        start = pl.multiple_of(where_ref[blocks + out], rows)
        total = 0.0
        for i, ref in enumerate(attn_refs):
            w = w_buf[i * part_heads : (i + 1) * part_heads].reshape(part_heads * HEAD_SIZE, columns)
            total = total + jnp.dot(ref[pl.ds(start, rows), :], w, preferred_element_type=jnp.float32)
        out_refs[out][...] = total.astype(jnp.bfloat16)


def project(where, attn, blocks, chunk, outs):
    count, _, heads, _, columns = blocks.shape
    rows = attn[0].shape[0] // outs
    vmem_spec = pl.BlockSpec(memory_space=pltpu.VMEM)
    return pl.pallas_call(
        functools.partial(project_kernel, len(attn), chunk, outs),
        in_specs=[pl.BlockSpec(memory_space=pltpu.SMEM)]
        + [vmem_spec] * len(attn)
        + [pl.BlockSpec(memory_space=pl.ANY)],
        out_specs=[vmem_spec] * outs,
        scratch_shapes=[
            pltpu.VMEM((heads, HEAD_SIZE, columns), jnp.bfloat16),
            pltpu.SemaphoreType.DMA((count,)),
        ],
        out_shape=[jax.ShapeDtypeStruct((rows, columns), jnp.bfloat16)] * outs,
        compiler_params=params(),
        cost_estimate=BRIEF,
        name="project",
    )(where, *attn, blocks)


def norm_kernel(chunks, gain_ref, *refs):
    out_ref = refs[-1]
    sums, square, column = [], 0.0, 0
    for i in range(chunks):
        total = refs[i][...].astype(jnp.float32) + refs[chunks + i][...].astype(jnp.float32)
        square = square + jnp.sum(total * total, axis=1, keepdims=True)
        sums.append(total)
    factor = lax.rsqrt(square / out_ref.shape[1] + 1e-06)
    for total in sums:
        width = total.shape[1]
        gain = gain_ref[:, column : column + width]
        out_ref[:, column : column + width] = (total * factor * gain).astype(jnp.bfloat16)
        column += width


def sum_and_norm(kept, arrived, post_gain):
    rows = kept[0].shape[0]
    block = min(128, rows)
    total = sum(a.shape[1] for a in kept)
    specs = [pl.BlockSpec((block, a.shape[1]), lambda i: (i, 0)) for a in kept + arrived]
    return pl.pallas_call(
        functools.partial(norm_kernel, len(kept)),
        grid=(rows // block,),
        in_specs=[pl.BlockSpec((1, total), lambda i: (0, 0))] + specs,
        out_specs=pl.BlockSpec((block, total), lambda i: (i, 0)),
        out_shape=jax.ShapeDtypeStruct((rows, total), jnp.bfloat16),
        compiler_params=params(),
        cost_estimate=BRIEF,
        name="sum_and_norm",
    )(post_gain.reshape(1, total), *kept, *arrived)


def ring_order(size):
    if size % 4:
        return list(range(size))
    up = [z * 4 + core for z in range(size // 4) for core in (0, 1)]
    down = [z * 4 + 2 + core for z in reversed(range(size // 4)) for core in (0, 1)]
    return up + down


def tie(values, after):
    if after is None:
        return values
    return lax.optimization_barrier((values, after))[0]


CHUNKS = ((3, 768), (2, 768))


def row_limits(ctx_index, tokens, doc_lengths):
    position = ctx_index * tokens + jnp.arange(tokens, dtype=jnp.int32)
    doc_ends = jnp.cumsum(doc_lengths)
    ended = doc_ends[None, :] <= position[:, None]
    doc_start = jnp.max(jnp.where(ended, doc_ends[None, :], 0), axis=1)
    low = jnp.maximum(position - (ATTEND_WINDOW - 1), doc_start) - ctx_index * tokens
    return jnp.broadcast_to(low[:, None], (tokens, 128))


def on_device(queries, rotated_key_rows, value_head_rows, w_out, post_gain, doc_lengths):
    tokens = queries.shape[0]
    heads = queries.shape[1] // HEAD_SIZE
    kv_heads = rotated_key_rows.shape[1] // HEAD_SIZE
    ctx_size, tp_size = lax.axis_size("ctx"), lax.axis_size("tp")
    tp_index = lax.axis_index("tp")
    rows = tokens // tp_size
    low = row_limits(lax.axis_index("ctx"), tokens, doc_lengths)

    near = (lax.axis_index("ctx") % 2).astype(jnp.int32)
    halos = []
    for head in range(kv_heads):
        cols = slice(head * HEAD_SIZE, (head + 1) * HEAD_SIZE)
        both = jnp.concatenate([rotated_key_rows[:, cols], value_head_rows[:, cols]], axis=1)
        chip = lax.ppermute(both, "ctx", [(i, i ^ 1) for i in range(ctx_size)])
        link = lax.ppermute(chip, "ctx", [(i, i + 2) for i in range(0, ctx_size - 2, 2)])
        halos.append((chip, link))

    attn = []
    for head in range(kv_heads):
        after = (halos[head], attn[-1]) if attn else halos[head]
        which = jnp.stack([near, jnp.int32(head)])
        attn.append(
            attend(which, tie(low, after), queries, rotated_key_rows, value_head_rows, halos[head], heads // kv_heads)
        )

    ring = ring_order(ctx_size)
    gathered, column = [], 0
    for chunks, width in CHUNKS:
        part = jnp.stack([w_out[:, :, column + i * width : column + (i + 1) * width] for i in range(chunks)])
        if len(gathered) == 1:
            part = tie(part, (attn[:-1], [link for _, link in halos]))
        gathered.append(lax.all_gather(part, "ctx", axis=0, tiled=False, axis_index_groups=[ring]))
        column += chunks * width

    kept, arrived = [], []
    starts = [(1 - tp_index) * rows, tp_index * rows] if tp_size == 2 else [jnp.int32(0)]
    where = jnp.stack([jnp.int32(i) for i in ring] + [i.astype(jnp.int32) for i in starts])
    for gather in gathered:
        for chunk in range(gather.shape[1]):
            number = len(kept)
            if number:
                where = tie(where, (kept[-1], arrived[max(number - 2, 0)] if number > 1 else ()))
            if tp_size == 2:
                send, keep = project(where, attn, gather, chunk, 2)
                arrived.append(lax.ppermute(send, "tp", [(0, 1), (1, 0)]))
            else:
                (keep,) = project(where, attn, gather, chunk, 1)
                if tp_size > 1:
                    keep = lax.psum_scatter(keep, "tp", scatter_dimension=0, tiled=True)
                arrived.append(jnp.zeros_like(keep))
            kept.append(keep)
    return sum_and_norm(kept, arrived, post_gain)


def solution(mesh):
    placed = (P("ctx", "tp"), P("ctx", "tp"), P("ctx", "tp"), P("tp", "ctx", None), P(), P())
    return jax.shard_map(
        on_device, mesh=mesh, in_specs=placed, out_specs=P(("ctx", "tp"), None), check_vma=False
    )
```

time: 244 us -> 208 us (0.85)
  waiting for transfers between devices: 134 us -> 89.1 us
  local copies, waits for them, and re-layouts: 7.22 us -> 20.9 us
  Pallas kernels: 73.7 us -> 64.4 us
  starting transfers between devices: 12.3 us -> 15.2 us
    ppermute x4 -> x5, waiting for transfers between devices: 54.8 us -> 31.3 us  [on_device(): arrived.append(lax.ppermute(send, 'tp', [(0, 1), (1, 0)]))]
    ppermute x4 -> x8, waiting for transfers between devices: 78.7 us -> 57.7 us  [the longest x4 56.5 us: on_device(): lax.ppermute(chip, 'ctx', [(i, i + 2) for i in range(0, ctx_size - 2, 2)])]
    unnamed x16 -> x52, local copies, waits for them, and re-layouts: 1.31 us -> 17.1 us
    pallas_call x8 -> x9, Pallas kernels: 67 us -> 59.5 us  [the longest x5 31.8 us: project(): pl.pallas_call(functools.partial(project_kernel, len(attn), chunk, outs),...]
    ppermute x4 -> x8, starting transfers between devices: 9.26 us -> 10.4 us  [the longest x4 9.15 us: on_device(): lax.ppermute(chip, 'ctx', [(i, i + 2) for i in range(0, ctx_size - 2, 2)])]
  transfers between devices with their start and end apart: 10 -> 15, of which waited for: 7 -> 9; matrix products, arithmetic and copies ran while one was open for 2% -> 2% of each run, Pallas kernels for 28% -> 29%
where the time goes in v3:
time: 208 us; the launch traced here: 207 us
  waiting for transfers between devices  89.1 us (43%)
  Pallas kernels  64.4 us (31%)
  local copies, waits for them, and re-layouts  20.9 us (10%)
  starting transfers between devices  15.2 us (7%)
  between operations  13.8 us (7%)
  other arithmetic  3.57 us (2%)
    ppermute x4, waiting for transfers between devices, on_device(): lax.ppermute(chip, 'ctx', [(i, i + 2) for i in range(0, ctx_size - 2, 2)])  56.5 us
    pallas_call x5, Pallas kernels, project(): pl.pallas_call(functools.partial(project_kernel, len(attn), chunk, outs),...  31.8 us
    ppermute x5, waiting for transfers between devices, on_device(): arrived.append(lax.ppermute(send, 'tp', [(0, 1), (1, 0)]))  31.3 us
    pallas_call x4, Pallas kernels, attend(): pl.pallas_call(functools.partial(attend_kernel, rows, groups), in_specs=[...  27.7 us
    unnamed x52, local copies, waits for them, and re-layouts  17.1 us
    ppermute x4, starting transfers between devices, on_device(): lax.ppermute(chip, 'ctx', [(i, i + 2) for i in range(0, ctx_size - 2, 2)])  9.15 us
    pallas_call x1, Pallas kernels, sum_and_norm(): pl.pallas_call(functools.partial(norm_kernel, len(kept)), grid=(rows // b...  4.82 us
    ppermute x5, starting transfers between devices, on_device(): arrived.append(lax.ppermute(send, 'tp', [(0, 1), (1, 0)]))  4.76 us
  transfers between devices with their start and end apart: 15, of which 9 were waited for; matrix products, arithmetic and copies ran while one was open for 2% of the time, Pallas kernels for 29%

profile of v3, /device:TPU:28, one launch (start us, length us, event | category | flops | bytes accessed | tf_op | source)
XLA Modules:
  0.0 206.9 jit_solution(7744384534996773558)
XLA Ops:
  9.0 1.9 fusion
  13.7 3.4 %collective-permute-start.1 = (bf16[1024,512]{1,0:T(8,128)(2,1)S(1)}, bf16[1024,512]{1,0:T(8,128)(2,1)}, u32[]{:S(2)}, u32[]{:S(2)}) collective-permute-start(bf16[1024,512]{1,0:T(8,128)(2,1)S(1)} %collective-permute-done.chip_ref), channel_id=1, source_target_pairs={{0,4},{4,8},{8,12},{12,16},{16,20},{20,24},{24,28},{1,5},{5,9},{9,... | collective-permute-start | bytes 3145736 | tf_op jit(solution)/shard_map/ppermute | solution.py:229
  17.1 1.9 collective-permute-start.3
  19.1 1.9 collective-permute-start.5
  21.0 1.9 collective-permute-start.7
  25.3 28.4 %collective-permute-done.1.link_ref = bf16[1024,512]{1,0:T(8,128)(2,1)} collective-permute-done((bf16[1024,512]{1,0:T(8,128)(2,1)S(1)}, bf16[1024,512]{1,0:T(8,128)(2,1)}, u32[]{:S(2)}, u32[]{:S(2)}) %collective-permute-start.1) | collective-permute-done | bytes 1048608 | tf_op jit(solution)/shard_map/ppermute | solution.py:229
  53.9 1.9 copy-done.1
  57.0 6.9 %attend.4.refs_0_ = bf16[1024,512]{1,0:T(8,128)(2,1)S(1)} custom-call(s32[2]{0:T(128)S(1)} %get-tuple-element.56.near_ref, s32[1024,128]{1,0:T(8,128)S(1)} %broadcast_in_dim.13.lo_ref, bf16[1024,2048]{1,0:T(8,128)(2,1)} %q_hbm.7, bf16[1024,1024]{1,0:T(8,128)(2,1)S(1)} %copy-done, bf16[1024,1024]{1,0:T(8,128)(2,1)S(1)} %copy-done.1, ...), custom_call_target="tpu_custom_call" | custom-call | flops 1 | bytes 1 | tf_op jit(solution)/shard_map/attend/pallas_call | solution.py:91
  63.9 21.5 %collective-permute-done.3.link_ref = bf16[1024,512]{1,0:T(8,128)(2,1)} collective-permute-done((bf16[1024,512]{1,0:T(8,128)(2,1)}, bf16[1024,512]{1,0:T(8,128)(2,1)}, u32[]{:S(2)}, u32[]{:S(2)}) %collective-permute-start.3) | collective-permute-done | bytes 1048608 | tf_op jit(solution)/shard_map/ppermute | solution.py:229
  85.4 6.9 %attend.5.refs_1_ = bf16[1024,512]{1,0:T(8,128)(2,1)S(1)} custom-call(s32[2]{0:T(128)S(1)} %get-tuple-element.57.near_ref, s32[1024,128]{1,0:T(8,128)S(1)} %broadcast_in_dim.13.lo_ref, bf16[1024,2048]{1,0:T(8,128)(2,1)} %q_hbm.7, bf16[1024,1024]{1,0:T(8,128)(2,1)S(1)} %copy-done, bf16[1024,1024]{1,0:T(8,128)(2,1)S(1)} %copy-done.1, ...), custom_call_target="tpu_custom_call" | custom-call | flops 1 | bytes 1 | tf_op jit(solution)/shard_map/attend/pallas_call | solution.py:91
  93.3 3.3 %collective-permute-done.5.link_ref = bf16[1024,512]{1,0:T(8,128)(2,1)} collective-permute-done((bf16[1024,512]{1,0:T(8,128)(2,1)}, bf16[1024,512]{1,0:T(8,128)(2,1)}, u32[]{:S(2)}, u32[]{:S(2)}) %collective-permute-start.5) | collective-permute-done | bytes 1048608 | tf_op jit(solution)/shard_map/ppermute | solution.py:229
  96.6 6.9 %attend.6.refs_2_ = bf16[1024,512]{1,0:T(8,128)(2,1)S(1)} custom-call(s32[2]{0:T(128)S(1)} %pad_add_fusion.2.near_ref, s32[1024,128]{1,0:T(8,128)S(1)} %broadcast_in_dim.13.lo_ref, bf16[1024,2048]{1,0:T(8,128)(2,1)} %q_hbm.7, bf16[1024,1024]{1,0:T(8,128)(2,1)S(1)} %copy-done, bf16[1024,1024]{1,0:T(8,128)(2,1)S(1)} %copy-done.1, ...), custom_call_target="tpu_custom_call" | custom-call | flops 1 | bytes 1 | tf_op jit(solution)/shard_map/attend/pallas_call | solution.py:91
  104.5 3.3 %collective-permute-done.7.link_ref = bf16[1024,512]{1,0:T(8,128)(2,1)} collective-permute-done((bf16[1024,512]{1,0:T(8,128)(2,1)}, bf16[1024,512]{1,0:T(8,128)(2,1)}, u32[]{:S(2)}, u32[]{:S(2)}) %collective-permute-start.7) | collective-permute-done | bytes 1048608 | tf_op jit(solution)/shard_map/ppermute | solution.py:229
  110.7 7.0 %attend.7.refs_3_ = bf16[1024,512]{1,0:T(8,128)(2,1)S(1)} custom-call(s32[2]{0:T(128)S(1)} %pad_add_fusion.3.near_ref, s32[1024,128]{1,0:T(8,128)S(1)} %copy-done.11, bf16[1024,2048]{1,0:T(8,128)(2,1)} %q_hbm.7, bf16[1024,1024]{1,0:T(8,128)(2,1)S(1)} %copy-done, bf16[1024,1024]{1,0:T(8,128)(2,1)S(1)} %copy-done.2, ...), custom_call_target="tpu_custom_call" | custom-call | flops 1 | bytes 1 | tf_op jit(solution)/shard_map/attend/pallas_call | solution.py:91
  122.4 6.1 %project.5 = (bf16[512,768]{1,0:T(8,128)(2,1)S(1)}, bf16[512,768]{1,0:T(8,128)(2,1)S(1)}) custom-call(s32[18]{0:T(128)S(1)} %stack.50.where_ref, bf16[1024,512]{1,0:T(8,128)(2,1)S(1)} %attend.4.refs_0_, bf16[1024,512]{1,0:T(8,128)(2,1)S(1)} %copy-done.4, bf16[1024,512]{1,0:T(8,128)(2,1)S(1)} %copy-done.6, bf16[1024,512]{1,0:T(8,128)(2,1)S(1)} %copy-done.8, ...), custom_call_target="tpu_custom_call" | custom-call | flops 1 | bytes 1 | tf_op jit(solution)/shard_map/project/pallas_call | solution.py:139
  129.9 6.1 %project.6 = (bf16[512,768]{1,0:T(8,128)(2,1)S(1)}, bf16[512,768]{1,0:T(8,128)(2,1)S(1)}) custom-call(s32[18]{0:T(128)S(1)} %stack.50.where_ref, bf16[1024,512]{1,0:T(8,128)(2,1)S(1)} %attend.4.refs_0_, bf16[1024,512]{1,0:T(8,128)(2,1)S(1)} %copy-done.4, bf16[1024,512]{1,0:T(8,128)(2,1)S(1)} %copy-done.6, bf16[1024,512]{1,0:T(8,128)(2,1)S(1)} %copy-done.8, ...), custom_call_target="tpu_custom_call" | custom-call | flops 1 | bytes 1 | tf_op jit(solution)/shard_map/project/pallas_call | solution.py:139
  138.4 2.9 %collective-permute-done.8.refs_5_ = bf16[512,768]{1,0:T(8,128)(2,1)S(1)} collective-permute-done((bf16[512,768]{1,0:T(8,128)(2,1)S(1)}, bf16[512,768]{1,0:T(8,128)(2,1)S(1)}, u32[]{:S(2)}, u32[]{:S(2)}) %collective-permute-start.8) | collective-permute-done | bytes 786464 | tf_op jit(solution)/shard_map/ppermute | solution.py:259
  141.4 7.0 %project.7 = (bf16[512,768]{1,0:T(8,128)(2,1)}, bf16[512,768]{1,0:T(8,128)(2,1)S(1)}) custom-call(s32[18]{0:T(128)S(1)} %stack.50.where_ref, bf16[1024,512]{1,0:T(8,128)(2,1)S(1)} %attend.4.refs_0_, bf16[1024,512]{1,0:T(8,128)(2,1)S(1)} %copy-done.4, bf16[1024,512]{1,0:T(8,128)(2,1)S(1)} %copy-done.6, bf16[1024,512]{1,0:T(8,128)(2,1)S(1)} %copy-done.8, ...), custom_call_target="tpu_custom_call" | custom-call | flops 1 | bytes 1 | tf_op jit(solution)/shard_map/project/pallas_call | solution.py:139
  152.0 6.3 %project.8 = (bf16[512,768]{1,0:T(8,128)(2,1)S(1)}, bf16[512,768]{1,0:T(8,128)(2,1)S(1)}) custom-call(s32[18]{0:T(128)S(1)} %stack.50.where_ref, bf16[1024,512]{1,0:T(8,128)(2,1)S(1)} %attend.4.refs_0_, bf16[1024,512]{1,0:T(8,128)(2,1)S(1)} %copy-done.4, bf16[1024,512]{1,0:T(8,128)(2,1)S(1)} %copy-done.6, bf16[1024,512]{1,0:T(8,128)(2,1)S(1)} %copy-done.9, ...), custom_call_target="tpu_custom_call" | custom-call | flops 1 | bytes 1 | tf_op jit(solution)/shard_map/project/pallas_call | solution.py:139
  159.8 5.0 %collective-permute-done.10.refs_7_ = bf16[512,768]{1,0:T(8,128)(2,1)} collective-permute-done((bf16[512,768]{1,0:T(8,128)(2,1)}, bf16[512,768]{1,0:T(8,128)(2,1)}, u32[]{:S(2)}, u32[]{:S(2)}) %collective-permute-start.10) | collective-permute-done | bytes 786464 | tf_op jit(solution)/shard_map/ppermute | solution.py:259
  164.9 6.3 %project.9 = (bf16[512,768]{1,0:T(8,128)(2,1)S(1)}, bf16[512,768]{1,0:T(8,128)(2,1)S(1)}) custom-call(s32[18]{0:T(128)S(1)} %stack.50.where_ref, bf16[1024,512]{1,0:T(8,128)(2,1)S(1)} %attend.4.refs_0_, bf16[1024,512]{1,0:T(8,128)(2,1)S(1)} %copy-done.4, bf16[1024,512]{1,0:T(8,128)(2,1)S(1)} %copy-done.6, bf16[1024,512]{1,0:T(8,128)(2,1)S(1)} %copy-done.9, ...), custom_call_target="tpu_custom_call" | custom-call | flops 1 | bytes 1 | tf_op jit(solution)/shard_map/project/pallas_call | solution.py:139
  171.9 9.7 %collective-permute-done.11.refs_8_ = bf16[512,768]{1,0:T(8,128)(2,1)S(1)} collective-permute-done((bf16[512,768]{1,0:T(8,128)(2,1)S(1)}, bf16[512,768]{1,0:T(8,128)(2,1)S(1)}, u32[]{:S(2)}, u32[]{:S(2)}) %collective-permute-start.11) | collective-permute-done | bytes 786464 | tf_op jit(solution)/shard_map/ppermute | solution.py:259
  181.6 13.6 %collective-permute-done.12.refs_9_ = bf16[512,768]{1,0:T(8,128)(2,1)S(1)} collective-permute-done((bf16[512,768]{1,0:T(8,128)(2,1)S(1)}, bf16[512,768]{1,0:T(8,128)(2,1)S(1)}, u32[]{:S(2)}, u32[]{:S(2)}) %collective-permute-start.12) | collective-permute-done | bytes 786464 | tf_op jit(solution)/shard_map/ppermute | solution.py:259
  195.2 4.8 %sum_and_norm.1 = bf16[512,3840]{1,0:T(8,128)(2,1)} custom-call(f32[1,3840]{1,0:T(1,128)S(1)} %reshape.38.gain_ref, bf16[512,768]{1,0:T(8,128)(2,1)S(1)} %copy-done.15, bf16[512,768]{1,0:T(8,128)(2,1)S(1)} %copy-done.19, bf16[512,768]{1,0:T(8,128)(2,1)S(1)} %copy-done.23, bf16[512,768]{1,0:T(8,128)(2,1)S(1)} %get-tuple-element.37.refs_3_, ...), custom_call_target="tpu_custom_call" | custom-call | flops 1 | bytes 1 | tf_op jit(solution)/shard_map/sum_and_norm/pallas_call | solution.py:176
  (90 shorter events, 28.0 us)
Async XLA Ops:
  6.5 112.2 %all-gather.5.cloned.1.call-start = ((), (), s32[]{:S(2)}) async-start(), calls=%async_computation | async-start | bytes 10027008 | tf_op jit(solution)/shard_map/all_gather | solution.py:246
  9.0 141.8 %all-gather.7.cloned.1.call-start = ((), (), s32[]{:S(2)}) async-start(), calls=%async_computation.1 | async-start | bytes 6684672 | tf_op jit(solution)/shard_map/all_gather | solution.py:246
  11.0 2.7 %collective-permute-start = (bf16[1024,512]{1,0:T(8,128)(2,1)S(1)}, bf16[1024,512]{1,0:T(8,128)(2,1)S(1)}, u32[]{:S(2)}, u32[]{:S(2)}) collective-permute-start(bf16[1024,512]{1,0:T(8,128)(2,1)S(1)} %pad_maximum_fusion), channel_id=1, source_target_pairs={{0,2},{2,0},{4,6},{6,4},{8,10},{10,8},{12,14},{14,12},{16,18},{18,... | collective-permute-start | bytes 3145736 | tf_op jit(solution)/shard_map/ppermute | solution.py:228
  11.2 6.0 %collective-permute-start.2 = (bf16[1024,512]{1,0:T(8,128)(2,1)S(1)}, bf16[1024,512]{1,0:T(8,128)(2,1)}, u32[]{:S(2)}, u32[]{:S(2)}) collective-permute-start(bf16[1024,512]{1,0:T(8,128)(2,1)S(1)} %pad_maximum_fusion.1), channel_id=1, source_target_pairs={{0,2},{2,0},{4,6},{6,4},{8,10},{10,8},{12,14},{14,12},{16,18},{18,... | collective-permute-start | bytes 3145736 | tf_op jit(solution)/shard_map/ppermute | solution.py:228
  11.7 11.2 %copy-start.25 = (s32[16]{0:T(128)S(1)}, s32[16]{0:T(128)}, u32[]{:S(2)}) copy-start(s32[16]{0:T(128)} %param.11) | copy-start | bytes 196
  11.8 7.3 %collective-permute-start.4 = (bf16[1024,512]{1,0:T(8,128)(2,1)S(1)}, bf16[1024,512]{1,0:T(8,128)(2,1)}, u32[]{:S(2)}, u32[]{:S(2)}) collective-permute-start(bf16[1024,512]{1,0:T(8,128)(2,1)S(1)} %pad_maximum_fusion.2), channel_id=1, source_target_pairs={{0,2},{2,0},{4,6},{6,4},{8,10},{10,8},{12,14},{14,12},{16,18},{18,... | collective-permute-start | bytes 3145736 | tf_op jit(solution)/shard_map/ppermute | solution.py:228
  12.0 9.0 %collective-permute-start.6 = (bf16[1024,512]{1,0:T(8,128)(2,1)S(1)}, bf16[1024,512]{1,0:T(8,128)(2,1)}, u32[]{:S(2)}, u32[]{:S(2)}) collective-permute-start(bf16[1024,512]{1,0:T(8,128)(2,1)S(1)} %pad_maximum_fusion.3), channel_id=1, source_target_pairs={{0,2},{2,0},{4,6},{6,4},{8,10},{10,8},{12,14},{14,12},{16,18},{18,... | collective-permute-start | bytes 3145736 | tf_op jit(solution)/shard_map/ppermute | solution.py:228
  13.7 40.2 %copy-start.12 = (bf16[1024,512]{1,0:T(8,128)(2,1)}, bf16[1024,512]{1,0:T(8,128)(2,1)S(1)}, u32[]{:S(2)}) copy-start(bf16[1024,512]{1,0:T(8,128)(2,1)S(1)} %collective-permute-done.chip_ref) | copy-start | bytes 3145732
  13.7 40.0 %collective-permute-start.1 = (bf16[1024,512]{1,0:T(8,128)(2,1)S(1)}, bf16[1024,512]{1,0:T(8,128)(2,1)}, u32[]{:S(2)}, u32[]{:S(2)}) collective-permute-start(bf16[1024,512]{1,0:T(8,128)(2,1)S(1)} %collective-permute-done.chip_ref), channel_id=1, source_target_pairs={{0,4},{4,8},{8,12},{12,16},{16,20},{20,24},{24,28},{1,5},{5,9},{9,... | collective-permute-start | bytes 3145736 | tf_op jit(solution)/shard_map/ppermute | solution.py:229
  17.1 68.3 %collective-permute-start.3 = (bf16[1024,512]{1,0:T(8,128)(2,1)}, bf16[1024,512]{1,0:T(8,128)(2,1)}, u32[]{:S(2)}, u32[]{:S(2)}) collective-permute-start(bf16[1024,512]{1,0:T(8,128)(2,1)} %collective-permute-done.2.chip_ref), channel_id=1, source_target_pairs={{0,4},{4,8},{8,12},{12,16},{16,20},{20,24},{24,28},{1,5},{5,9},{9,... | collective-permute-start | bytes 3145736 | tf_op jit(solution)/shard_map/ppermute | solution.py:229
  19.1 77.6 %collective-permute-start.5 = (bf16[1024,512]{1,0:T(8,128)(2,1)}, bf16[1024,512]{1,0:T(8,128)(2,1)}, u32[]{:S(2)}, u32[]{:S(2)}) collective-permute-start(bf16[1024,512]{1,0:T(8,128)(2,1)} %collective-permute-done.4.chip_ref), channel_id=1, source_target_pairs={{0,4},{4,8},{8,12},{12,16},{16,20},{20,24},{24,28},{1,5},{5,9},{9,... | collective-permute-start | bytes 3145736 | tf_op jit(solution)/shard_map/ppermute | solution.py:229
  21.0 86.9 %collective-permute-start.7 = (bf16[1024,512]{1,0:T(8,128)(2,1)}, bf16[1024,512]{1,0:T(8,128)(2,1)}, u32[]{:S(2)}, u32[]{:S(2)}) collective-permute-start(bf16[1024,512]{1,0:T(8,128)(2,1)} %collective-permute-done.6.chip_ref), channel_id=1, source_target_pairs={{0,4},{4,8},{8,12},{12,16},{16,20},{20,24},{24,28},{1,5},{5,9},{9,... | collective-permute-start | bytes 3145736 | tf_op jit(solution)/shard_map/ppermute | solution.py:229
  53.9 42.7 %copy-start.10 = (s32[1024,128]{1,0:T(8,128)}, s32[1024,128]{1,0:T(8,128)S(1)}, u32[]{:S(2)}) copy-start(s32[1024,128]{1,0:T(8,128)S(1)} %broadcast_in_dim.13.lo_ref) | copy-start | bytes 1572868
  129.4 12.0 %collective-permute-start.8 = (bf16[512,768]{1,0:T(8,128)(2,1)S(1)}, bf16[512,768]{1,0:T(8,128)(2,1)S(1)}, u32[]{:S(2)}, u32[]{:S(2)}) collective-permute-start(bf16[512,768]{1,0:T(8,128)(2,1)S(1)} %get-tuple-element.31), channel_id=1, source_target_pairs={{0,1},{1,0},{2,3},{3,2},{4,5},{5,4},{6,7},{7,6},{8,9},{9,8},{10,11... | collective-permute-start | bytes 2359304 | tf_op jit(solution)/shard_map/ppermute | solution.py:259
  137.0 12.9 %collective-permute-start.9 = (bf16[512,768]{1,0:T(8,128)(2,1)S(1)}, bf16[512,768]{1,0:T(8,128)(2,1)S(1)}, u32[]{:S(2)}, u32[]{:S(2)}) collective-permute-start(bf16[512,768]{1,0:T(8,128)(2,1)S(1)} %get-tuple-element.34), channel_id=1, source_target_pairs={{0,1},{1,0},{2,3},{3,2},{4,5},{5,4},{6,7},{7,6},{8,9},{9,8},{10,11... | collective-permute-start | bytes 2359304 | tf_op jit(solution)/shard_map/ppermute | solution.py:259
  141.4 7.0 %copy-start.16 = (bf16[512,768]{1,0:T(8,128)(2,1)}, bf16[512,768]{1,0:T(8,128)(2,1)S(1)}, u32[]{:S(2)}) copy-start(bf16[512,768]{1,0:T(8,128)(2,1)S(1)} %collective-permute-done.8.refs_5_) | copy-start | bytes 2359300
  149.3 15.5 %collective-permute-start.10 = (bf16[512,768]{1,0:T(8,128)(2,1)}, bf16[512,768]{1,0:T(8,128)(2,1)}, u32[]{:S(2)}, u32[]{:S(2)}) collective-permute-start(bf16[512,768]{1,0:T(8,128)(2,1)} %get-tuple-element.38), channel_id=1, source_target_pairs={{0,1},{1,0},{2,3},{3,2},{4,5},{5,4},{6,7},{7,6},{8,9},{9,8},{10,11... | collective-permute-start | bytes 2359304 | tf_op jit(solution)/shard_map/ppermute | solution.py:259
  158.3 23.3 %collective-permute-start.11 = (bf16[512,768]{1,0:T(8,128)(2,1)S(1)}, bf16[512,768]{1,0:T(8,128)(2,1)S(1)}, u32[]{:S(2)}, u32[]{:S(2)}) collective-permute-start(bf16[512,768]{1,0:T(8,128)(2,1)S(1)} %get-tuple-element.41), channel_id=1, source_target_pairs={{0,1},{1,0},{2,3},{3,2},{4,5},{5,4},{6,7},{7,6},{8,9},{9,8},{10,11... | collective-permute-start | bytes 2359304 | tf_op jit(solution)/shard_map/ppermute | solution.py:259
  164.8 30.4 %copy-start.15 = (bf16[512,768]{1,0:T(8,128)(2,1)S(1)}, bf16[512,768]{1,0:T(8,128)(2,1)}, u32[]{:S(2)}) copy-start(bf16[512,768]{1,0:T(8,128)(2,1)} %copy-done.14) | copy-start | bytes 2359300
  164.8 30.4 %copy-start.17 = (bf16[512,768]{1,0:T(8,128)(2,1)S(1)}, bf16[512,768]{1,0:T(8,128)(2,1)}, u32[]{:S(2)}) copy-start(bf16[512,768]{1,0:T(8,128)(2,1)} %copy-done.16) | copy-start | bytes 2359300
  164.8 30.4 %copy-start.19 = (bf16[512,768]{1,0:T(8,128)(2,1)S(1)}, bf16[512,768]{1,0:T(8,128)(2,1)}, u32[]{:S(2)}) copy-start(bf16[512,768]{1,0:T(8,128)(2,1)} %copy-done.18) | copy-start | bytes 2359300
  164.8 30.4 %copy-start.21 = (bf16[512,768]{1,0:T(8,128)(2,1)S(1)}, bf16[512,768]{1,0:T(8,128)(2,1)}, u32[]{:S(2)}) copy-start(bf16[512,768]{1,0:T(8,128)(2,1)} %copy-done.20) | copy-start | bytes 2359300
  164.9 30.4 %copy-start.23 = (bf16[512,768]{1,0:T(8,128)(2,1)S(1)}, bf16[512,768]{1,0:T(8,128)(2,1)}, u32[]{:S(2)}) copy-start(bf16[512,768]{1,0:T(8,128)(2,1)} %copy-done.22) | copy-start | bytes 2359300
  171.2 24.0 %collective-permute-start.12 = (bf16[512,768]{1,0:T(8,128)(2,1)S(1)}, bf16[512,768]{1,0:T(8,128)(2,1)S(1)}, u32[]{:S(2)}, u32[]{:S(2)}) collective-permute-start(bf16[512,768]{1,0:T(8,128)(2,1)S(1)} %get-tuple-element.42), channel_id=1, source_target_pairs={{0,1},{1,0},{2,3},{3,2},{4,5},{5,4},{6,7},{7,6},{8,9},{9,8},{10,11... | collective-permute-start | bytes 2359304 | tf_op jit(solution)/shard_map/ppermute | solution.py:259
  (17 other events, 26.6 us)
Sparse Core Ops, SparseCore 0:
  9.1 77.1 all-gather.4
  108.0 39.6 all-gather.6

commit v4 on v3

--- a/solution.py
+++ b/solution.py
@@ -253,7 +253,7 @@
         for chunk in range(gather.shape[1]):
             number = len(kept)
             if number:
-                where = tie(where, (kept[-1], arrived[max(number - 2, 0)] if number > 1 else ()))
+                where = tie(where, (kept[-1], arrived[number - 3] if number > 2 else ()))
             if tp_size == 2:
                 send, keep = project(where, attn, gather, chunk, 2)
                 arrived.append(lax.ppermute(send, "tp", [(0, 1), (1, 0)]))

time: 208 us -> 207 us (level)
  waiting for transfers between devices: 89.1 us -> 86.4 us
    ppermute x5, waiting for transfers between devices: 31.3 us -> 28.6 us  [on_device(): arrived.append(lax.ppermute(send, 'tp', [(0, 1), (1, 0)]))]
    unnamed x52 -> x48, local copies, waits for them, and re-layouts: 17.1 us -> 17.1 us
  transfers between devices with their start and end apart: 15 -> 15, of which waited for: 9 -> 7; matrix products, arithmetic and copies ran while one was open for 2% -> 2% of each run, Pallas kernels for 29% -> 29%
where the time goes in v4:
time: 207 us; the launch traced here: 205 us
  waiting for transfers between devices  86.4 us (42%)
  Pallas kernels  65.2 us (31%)
  local copies, waits for them, and re-layouts  20.9 us (10%)
  starting transfers between devices  15.2 us (7%)
  between operations  13.8 us (7%)
  other arithmetic  3.6 us (2%)
    ppermute x4, waiting for transfers between devices, on_device(): lax.ppermute(chip, 'ctx', [(i, i + 2) for i in range(0, ctx_size - 2, 2)])  56.5 us
    pallas_call x5, Pallas kernels, project(): pl.pallas_call(functools.partial(project_kernel, len(attn), chunk, outs),...  32.4 us
    ppermute x5, waiting for transfers between devices, on_device(): arrived.append(lax.ppermute(send, 'tp', [(0, 1), (1, 0)]))  28.6 us
    pallas_call x4, Pallas kernels, attend(): pl.pallas_call(functools.partial(attend_kernel, rows, groups), in_specs=[...  27.7 us
    unnamed x48, local copies, waits for them, and re-layouts  17.1 us
    ppermute x4, starting transfers between devices, on_device(): lax.ppermute(chip, 'ctx', [(i, i + 2) for i in range(0, ctx_size - 2, 2)])  9.15 us
    pallas_call x1, Pallas kernels, sum_and_norm(): pl.pallas_call(functools.partial(norm_kernel, len(kept)), grid=(rows // b...  5.03 us
    ppermute x5, starting transfers between devices, on_device(): arrived.append(lax.ppermute(send, 'tp', [(0, 1), (1, 0)]))  4.74 us
  transfers between devices with their start and end apart: 15, of which 7 were waited for; matrix products, arithmetic and copies ran while one was open for 2% of the time, Pallas kernels for 29%

profile of v4, /device:TPU:28, one launch (start us, length us, event | category | flops | bytes accessed | tf_op | source)
XLA Modules:
  0.0 205.0 jit_solution(10747309873045988448)
XLA Ops:
  9.0 1.9 fusion
  13.7 3.4 %collective-permute-start.1 = (bf16[1024,512]{1,0:T(8,128)(2,1)S(1)}, bf16[1024,512]{1,0:T(8,128)(2,1)}, u32[]{:S(2)}, u32[]{:S(2)}) collective-permute-start(bf16[1024,512]{1,0:T(8,128)(2,1)S(1)} %collective-permute-done.chip_ref), channel_id=1, source_target_pairs={{0,4},{4,8},{8,12},{12,16},{16,20},{20,24},{24,28},{1,5},{5,9},{9,... | collective-permute-start | bytes 3145736 | tf_op jit(solution)/shard_map/ppermute | solution.py:229
  17.1 1.9 collective-permute-start.3
  19.1 1.9 collective-permute-start.5
  21.0 1.9 collective-permute-start.7
  25.4 28.3 %collective-permute-done.1.link_ref = bf16[1024,512]{1,0:T(8,128)(2,1)} collective-permute-done((bf16[1024,512]{1,0:T(8,128)(2,1)S(1)}, bf16[1024,512]{1,0:T(8,128)(2,1)}, u32[]{:S(2)}, u32[]{:S(2)}) %collective-permute-start.1) | collective-permute-done | bytes 1048608 | tf_op jit(solution)/shard_map/ppermute | solution.py:229
  53.9 1.9 copy-done.1
  57.0 6.9 %attend.4.refs_0_ = bf16[1024,512]{1,0:T(8,128)(2,1)S(1)} custom-call(s32[2]{0:T(128)S(1)} %get-tuple-element.56.near_ref, s32[1024,128]{1,0:T(8,128)S(1)} %broadcast_in_dim.13.lo_ref, bf16[1024,2048]{1,0:T(8,128)(2,1)} %q_hbm.7, bf16[1024,1024]{1,0:T(8,128)(2,1)S(1)} %copy-done, bf16[1024,1024]{1,0:T(8,128)(2,1)S(1)} %copy-done.1, ...), custom_call_target="tpu_custom_call" | custom-call | flops 1 | bytes 1 | tf_op jit(solution)/shard_map/attend/pallas_call | solution.py:91
  63.9 21.5 %collective-permute-done.3.link_ref = bf16[1024,512]{1,0:T(8,128)(2,1)} collective-permute-done((bf16[1024,512]{1,0:T(8,128)(2,1)}, bf16[1024,512]{1,0:T(8,128)(2,1)}, u32[]{:S(2)}, u32[]{:S(2)}) %collective-permute-start.3) | collective-permute-done | bytes 1048608 | tf_op jit(solution)/shard_map/ppermute | solution.py:229
  85.4 6.9 %attend.5.refs_1_ = bf16[1024,512]{1,0:T(8,128)(2,1)S(1)} custom-call(s32[2]{0:T(128)S(1)} %get-tuple-element.57.near_ref, s32[1024,128]{1,0:T(8,128)S(1)} %broadcast_in_dim.13.lo_ref, bf16[1024,2048]{1,0:T(8,128)(2,1)} %q_hbm.7, bf16[1024,1024]{1,0:T(8,128)(2,1)S(1)} %copy-done, bf16[1024,1024]{1,0:T(8,128)(2,1)S(1)} %copy-done.1, ...), custom_call_target="tpu_custom_call" | custom-call | flops 1 | bytes 1 | tf_op jit(solution)/shard_map/attend/pallas_call | solution.py:91
  93.3 3.3 %collective-permute-done.5.link_ref = bf16[1024,512]{1,0:T(8,128)(2,1)} collective-permute-done((bf16[1024,512]{1,0:T(8,128)(2,1)}, bf16[1024,512]{1,0:T(8,128)(2,1)}, u32[]{:S(2)}, u32[]{:S(2)}) %collective-permute-start.5) | collective-permute-done | bytes 1048608 | tf_op jit(solution)/shard_map/ppermute | solution.py:229
  96.6 6.9 %attend.6.refs_2_ = bf16[1024,512]{1,0:T(8,128)(2,1)S(1)} custom-call(s32[2]{0:T(128)S(1)} %pad_add_fusion.2.near_ref, s32[1024,128]{1,0:T(8,128)S(1)} %broadcast_in_dim.13.lo_ref, bf16[1024,2048]{1,0:T(8,128)(2,1)} %q_hbm.7, bf16[1024,1024]{1,0:T(8,128)(2,1)S(1)} %copy-done, bf16[1024,1024]{1,0:T(8,128)(2,1)S(1)} %copy-done.1, ...), custom_call_target="tpu_custom_call" | custom-call | flops 1 | bytes 1 | tf_op jit(solution)/shard_map/attend/pallas_call | solution.py:91
  104.5 3.4 %collective-permute-done.7.link_ref = bf16[1024,512]{1,0:T(8,128)(2,1)} collective-permute-done((bf16[1024,512]{1,0:T(8,128)(2,1)}, bf16[1024,512]{1,0:T(8,128)(2,1)}, u32[]{:S(2)}, u32[]{:S(2)}) %collective-permute-start.7) | collective-permute-done | bytes 1048608 | tf_op jit(solution)/shard_map/ppermute | solution.py:229
  108.1 1.6 copy-done.2
  110.7 7.0 %attend.7.refs_3_ = bf16[1024,512]{1,0:T(8,128)(2,1)S(1)} custom-call(s32[2]{0:T(128)S(1)} %pad_add_fusion.3.near_ref, s32[1024,128]{1,0:T(8,128)S(1)} %copy-done.11, bf16[1024,2048]{1,0:T(8,128)(2,1)} %q_hbm.7, bf16[1024,1024]{1,0:T(8,128)(2,1)S(1)} %copy-done, bf16[1024,1024]{1,0:T(8,128)(2,1)S(1)} %copy-done.2, ...), custom_call_target="tpu_custom_call" | custom-call | flops 1 | bytes 1 | tf_op jit(solution)/shard_map/attend/pallas_call | solution.py:91
  122.4 6.1 %project.5 = (bf16[512,768]{1,0:T(8,128)(2,1)S(1)}, bf16[512,768]{1,0:T(8,128)(2,1)S(1)}) custom-call(s32[18]{0:T(128)S(1)} %stack.50.where_ref, bf16[1024,512]{1,0:T(8,128)(2,1)S(1)} %attend.4.refs_0_, bf16[1024,512]{1,0:T(8,128)(2,1)S(1)} %copy-done.4, bf16[1024,512]{1,0:T(8,128)(2,1)S(1)} %copy-done.6, bf16[1024,512]{1,0:T(8,128)(2,1)S(1)} %copy-done.8, ...), custom_call_target="tpu_custom_call" | custom-call | flops 1 | bytes 1 | tf_op jit(solution)/shard_map/project/pallas_call | solution.py:139
  129.9 7.0 %project.6 = (bf16[512,768]{1,0:T(8,128)(2,1)}, bf16[512,768]{1,0:T(8,128)(2,1)S(1)}) custom-call(s32[18]{0:T(128)S(1)} %stack.50.where_ref, bf16[1024,512]{1,0:T(8,128)(2,1)S(1)} %attend.4.refs_0_, bf16[1024,512]{1,0:T(8,128)(2,1)S(1)} %copy-done.4, bf16[1024,512]{1,0:T(8,128)(2,1)S(1)} %copy-done.6, bf16[1024,512]{1,0:T(8,128)(2,1)S(1)} %copy-done.8, ...), custom_call_target="tpu_custom_call" | custom-call | flops 1 | bytes 1 | tf_op jit(solution)/shard_map/project/pallas_call | solution.py:139
  139.3 7.0 %project.7 = (bf16[512,768]{1,0:T(8,128)(2,1)}, bf16[512,768]{1,0:T(8,128)(2,1)S(1)}) custom-call(s32[18]{0:T(128)S(1)} %stack.50.where_ref, bf16[1024,512]{1,0:T(8,128)(2,1)S(1)} %attend.4.refs_0_, bf16[1024,512]{1,0:T(8,128)(2,1)S(1)} %copy-done.4, bf16[1024,512]{1,0:T(8,128)(2,1)S(1)} %copy-done.6, bf16[1024,512]{1,0:T(8,128)(2,1)S(1)} %copy-done.8, ...), custom_call_target="tpu_custom_call" | custom-call | flops 1 | bytes 1 | tf_op jit(solution)/shard_map/project/pallas_call | solution.py:139
  149.9 6.3 %project.8 = (bf16[512,768]{1,0:T(8,128)(2,1)S(1)}, bf16[512,768]{1,0:T(8,128)(2,1)S(1)}) custom-call(s32[18]{0:T(128)S(1)} %stack.50.where_ref, bf16[1024,512]{1,0:T(8,128)(2,1)S(1)} %attend.4.refs_0_, bf16[1024,512]{1,0:T(8,128)(2,1)S(1)} %copy-done.4, bf16[1024,512]{1,0:T(8,128)(2,1)S(1)} %copy-done.6, bf16[1024,512]{1,0:T(8,128)(2,1)S(1)} %copy-done.9, ...), custom_call_target="tpu_custom_call" | custom-call | flops 1 | bytes 1 | tf_op jit(solution)/shard_map/project/pallas_call | solution.py:139
  156.2 1.5 collective-permute-start.11
  157.8 6.0 %project.9 = (bf16[512,768]{1,0:T(8,128)(2,1)S(1)}, bf16[512,768]{1,0:T(8,128)(2,1)S(1)}) custom-call(s32[18]{0:T(128)S(1)} %stack.50.where_ref, bf16[1024,512]{1,0:T(8,128)(2,1)S(1)} %attend.4.refs_0_, bf16[1024,512]{1,0:T(8,128)(2,1)S(1)} %copy-done.4, bf16[1024,512]{1,0:T(8,128)(2,1)S(1)} %copy-done.6, bf16[1024,512]{1,0:T(8,128)(2,1)S(1)} %copy-done.9, ...), custom_call_target="tpu_custom_call" | custom-call | flops 1 | bytes 1 | tf_op jit(solution)/shard_map/project/pallas_call | solution.py:139
  164.5 12.9 %collective-permute-done.11.refs_8_ = bf16[512,768]{1,0:T(8,128)(2,1)S(1)} collective-permute-done((bf16[512,768]{1,0:T(8,128)(2,1)S(1)}, bf16[512,768]{1,0:T(8,128)(2,1)S(1)}, u32[]{:S(2)}, u32[]{:S(2)}) %collective-permute-start.11) | collective-permute-done | bytes 786464 | tf_op jit(solution)/shard_map/ppermute | solution.py:259
  177.4 15.8 %collective-permute-done.12.refs_9_ = bf16[512,768]{1,0:T(8,128)(2,1)S(1)} collective-permute-done((bf16[512,768]{1,0:T(8,128)(2,1)S(1)}, bf16[512,768]{1,0:T(8,128)(2,1)S(1)}, u32[]{:S(2)}, u32[]{:S(2)}) %collective-permute-start.12) | collective-permute-done | bytes 786464 | tf_op jit(solution)/shard_map/ppermute | solution.py:259
  193.1 5.0 %sum_and_norm.1 = bf16[512,3840]{1,0:T(8,128)(2,1)} custom-call(f32[1,3840]{1,0:T(1,128)S(1)} %reshape.38.gain_ref, bf16[512,768]{1,0:T(8,128)(2,1)S(1)} %copy-done.15, bf16[512,768]{1,0:T(8,128)(2,1)S(1)} %copy-done.19, bf16[512,768]{1,0:T(8,128)(2,1)S(1)} %copy-done.21, bf16[512,768]{1,0:T(8,128)(2,1)S(1)} %get-tuple-element.36.refs_3_, ...), custom_call_target="tpu_custom_call" | custom-call | flops 1 | bytes 1 | tf_op jit(solution)/shard_map/sum_and_norm/pallas_call | solution.py:176
  (86 shorter events, 24.9 us)
Async XLA Ops:
  6.5 2.5 %copy-start = (bf16[1024,1024]{1,0:T(8,128)(2,1)S(1)}, bf16[1024,1024]{1,0:T(8,128)(2,1)}, u32[]{:S(2)}) copy-start(bf16[1024,1024]{1,0:T(8,128)(2,1)} %k_hbm.7) | copy-start | bytes 6291460
  6.5 112.2 %all-gather.5.cloned.1.call-start = ((), (), s32[]{:S(2)}) async-start(), calls=%async_computation | async-start | bytes 10027008 | tf_op jit(solution)/shard_map/all_gather | solution.py:246
  9.0 139.7 %all-gather.7.cloned.1.call-start = ((), (), s32[]{:S(2)}) async-start(), calls=%async_computation.1 | async-start | bytes 6684672 | tf_op jit(solution)/shard_map/all_gather | solution.py:246
  11.0 2.7 %collective-permute-start = (bf16[1024,512]{1,0:T(8,128)(2,1)S(1)}, bf16[1024,512]{1,0:T(8,128)(2,1)S(1)}, u32[]{:S(2)}, u32[]{:S(2)}) collective-permute-start(bf16[1024,512]{1,0:T(8,128)(2,1)S(1)} %pad_maximum_fusion), channel_id=1, source_target_pairs={{0,2},{2,0},{4,6},{6,4},{8,10},{10,8},{12,14},{14,12},{16,18},{18,... | collective-permute-start | bytes 3145736 | tf_op jit(solution)/shard_map/ppermute | solution.py:228
  11.1 6.0 %collective-permute-start.2 = (bf16[1024,512]{1,0:T(8,128)(2,1)S(1)}, bf16[1024,512]{1,0:T(8,128)(2,1)}, u32[]{:S(2)}, u32[]{:S(2)}) collective-permute-start(bf16[1024,512]{1,0:T(8,128)(2,1)S(1)} %pad_maximum_fusion.1), channel_id=1, source_target_pairs={{0,2},{2,0},{4,6},{6,4},{8,10},{10,8},{12,14},{14,12},{16,18},{18,... | collective-permute-start | bytes 3145736 | tf_op jit(solution)/shard_map/ppermute | solution.py:228
  11.7 11.2 %copy-start.23 = (s32[16]{0:T(128)S(1)}, s32[16]{0:T(128)}, u32[]{:S(2)}) copy-start(s32[16]{0:T(128)} %param.11) | copy-start | bytes 196
  11.8 7.3 %collective-permute-start.4 = (bf16[1024,512]{1,0:T(8,128)(2,1)S(1)}, bf16[1024,512]{1,0:T(8,128)(2,1)}, u32[]{:S(2)}, u32[]{:S(2)}) collective-permute-start(bf16[1024,512]{1,0:T(8,128)(2,1)S(1)} %pad_maximum_fusion.2), channel_id=1, source_target_pairs={{0,2},{2,0},{4,6},{6,4},{8,10},{10,8},{12,14},{14,12},{16,18},{18,... | collective-permute-start | bytes 3145736 | tf_op jit(solution)/shard_map/ppermute | solution.py:228
  12.0 9.0 %collective-permute-start.6 = (bf16[1024,512]{1,0:T(8,128)(2,1)S(1)}, bf16[1024,512]{1,0:T(8,128)(2,1)}, u32[]{:S(2)}, u32[]{:S(2)}) collective-permute-start(bf16[1024,512]{1,0:T(8,128)(2,1)S(1)} %pad_maximum_fusion.3), channel_id=1, source_target_pairs={{0,2},{2,0},{4,6},{6,4},{8,10},{10,8},{12,14},{14,12},{16,18},{18,... | collective-permute-start | bytes 3145736 | tf_op jit(solution)/shard_map/ppermute | solution.py:228
  13.7 40.2 %copy-start.12 = (bf16[1024,512]{1,0:T(8,128)(2,1)}, bf16[1024,512]{1,0:T(8,128)(2,1)S(1)}, u32[]{:S(2)}) copy-start(bf16[1024,512]{1,0:T(8,128)(2,1)S(1)} %collective-permute-done.chip_ref) | copy-start | bytes 3145732
  13.7 40.0 %collective-permute-start.1 = (bf16[1024,512]{1,0:T(8,128)(2,1)S(1)}, bf16[1024,512]{1,0:T(8,128)(2,1)}, u32[]{:S(2)}, u32[]{:S(2)}) collective-permute-start(bf16[1024,512]{1,0:T(8,128)(2,1)S(1)} %collective-permute-done.chip_ref), channel_id=1, source_target_pairs={{0,4},{4,8},{8,12},{12,16},{16,20},{20,24},{24,28},{1,5},{5,9},{9,... | collective-permute-start | bytes 3145736 | tf_op jit(solution)/shard_map/ppermute | solution.py:229
  17.1 68.3 %collective-permute-start.3 = (bf16[1024,512]{1,0:T(8,128)(2,1)}, bf16[1024,512]{1,0:T(8,128)(2,1)}, u32[]{:S(2)}, u32[]{:S(2)}) collective-permute-start(bf16[1024,512]{1,0:T(8,128)(2,1)} %collective-permute-done.2.chip_ref), channel_id=1, source_target_pairs={{0,4},{4,8},{8,12},{12,16},{16,20},{20,24},{24,28},{1,5},{5,9},{9,... | collective-permute-start | bytes 3145736 | tf_op jit(solution)/shard_map/ppermute | solution.py:229
  19.1 77.6 %collective-permute-start.5 = (bf16[1024,512]{1,0:T(8,128)(2,1)}, bf16[1024,512]{1,0:T(8,128)(2,1)}, u32[]{:S(2)}, u32[]{:S(2)}) collective-permute-start(bf16[1024,512]{1,0:T(8,128)(2,1)} %collective-permute-done.4.chip_ref), channel_id=1, source_target_pairs={{0,4},{4,8},{8,12},{12,16},{16,20},{20,24},{24,28},{1,5},{5,9},{9,... | collective-permute-start | bytes 3145736 | tf_op jit(solution)/shard_map/ppermute | solution.py:229
  21.0 86.9 %collective-permute-start.7 = (bf16[1024,512]{1,0:T(8,128)(2,1)}, bf16[1024,512]{1,0:T(8,128)(2,1)}, u32[]{:S(2)}, u32[]{:S(2)}) collective-permute-start(bf16[1024,512]{1,0:T(8,128)(2,1)} %collective-permute-done.6.chip_ref), channel_id=1, source_target_pairs={{0,4},{4,8},{8,12},{12,16},{16,20},{20,24},{24,28},{1,5},{5,9},{9,... | collective-permute-start | bytes 3145736 | tf_op jit(solution)/shard_map/ppermute | solution.py:229
  53.9 42.7 %copy-start.10 = (s32[1024,128]{1,0:T(8,128)}, s32[1024,128]{1,0:T(8,128)S(1)}, u32[]{:S(2)}) copy-start(s32[1024,128]{1,0:T(8,128)S(1)} %broadcast_in_dim.13.lo_ref) | copy-start | bytes 1572868
  129.4 18.4 %collective-permute-start.8 = (bf16[512,768]{1,0:T(8,128)(2,1)S(1)}, bf16[512,768]{1,0:T(8,128)(2,1)S(1)}, u32[]{:S(2)}, u32[]{:S(2)}) collective-permute-start(bf16[512,768]{1,0:T(8,128)(2,1)S(1)} %get-tuple-element.33), channel_id=1, source_target_pairs={{0,1},{1,0},{2,3},{3,2},{4,5},{5,4},{6,7},{7,6},{8,9},{9,8},{10,11... | collective-permute-start | bytes 2359304 | tf_op jit(solution)/shard_map/ppermute | solution.py:259
  137.8 18.3 %collective-permute-start.9 = (bf16[512,768]{1,0:T(8,128)(2,1)}, bf16[512,768]{1,0:T(8,128)(2,1)}, u32[]{:S(2)}, u32[]{:S(2)}) collective-permute-start(bf16[512,768]{1,0:T(8,128)(2,1)} %get-tuple-element.37), channel_id=1, source_target_pairs={{0,1},{1,0},{2,3},{3,2},{4,5},{5,4},{6,7},{7,6},{8,9},{9,8},{10,11... | collective-permute-start | bytes 2359304 | tf_op jit(solution)/shard_map/ppermute | solution.py:259
  147.2 17.3 %collective-permute-start.10 = (bf16[512,768]{1,0:T(8,128)(2,1)}, bf16[512,768]{1,0:T(8,128)(2,1)}, u32[]{:S(2)}, u32[]{:S(2)}) collective-permute-start(bf16[512,768]{1,0:T(8,128)(2,1)} %get-tuple-element.40), channel_id=1, source_target_pairs={{0,1},{1,0},{2,3},{3,2},{4,5},{5,4},{6,7},{7,6},{8,9},{9,8},{10,11... | collective-permute-start | bytes 2359304 | tf_op jit(solution)/shard_map/ppermute | solution.py:259
  156.2 8.3 %copy-start.22 = (f32[3840]{0:T(1024)S(1)}, f32[3840]{0:T(1024)}, u32[]{:S(2)}) copy-start(f32[3840]{0:T(1024)} %param.10) | copy-start | bytes 46084
  156.2 36.9 %copy-start.15 = (bf16[512,768]{1,0:T(8,128)(2,1)S(1)}, bf16[512,768]{1,0:T(8,128)(2,1)}, u32[]{:S(2)}) copy-start(bf16[512,768]{1,0:T(8,128)(2,1)} %copy-done.14) | copy-start | bytes 2359300
  156.2 36.9 %copy-start.17 = (bf16[512,768]{1,0:T(8,128)(2,1)S(1)}, bf16[512,768]{1,0:T(8,128)(2,1)}, u32[]{:S(2)}) copy-start(bf16[512,768]{1,0:T(8,128)(2,1)} %copy-done.16) | copy-start | bytes 2359300
  156.2 36.9 %copy-start.19 = (bf16[512,768]{1,0:T(8,128)(2,1)S(1)}, bf16[512,768]{1,0:T(8,128)(2,1)}, u32[]{:S(2)}) copy-start(bf16[512,768]{1,0:T(8,128)(2,1)} %copy-done.18) | copy-start | bytes 2359300
  156.2 36.9 %copy-start.21 = (bf16[512,768]{1,0:T(8,128)(2,1)S(1)}, bf16[512,768]{1,0:T(8,128)(2,1)}, u32[]{:S(2)}) copy-start(bf16[512,768]{1,0:T(8,128)(2,1)} %copy-done.20) | copy-start | bytes 2359300
  156.2 21.1 %collective-permute-start.11 = (bf16[512,768]{1,0:T(8,128)(2,1)S(1)}, bf16[512,768]{1,0:T(8,128)(2,1)S(1)}, u32[]{:S(2)}, u32[]{:S(2)}) collective-permute-start(bf16[512,768]{1,0:T(8,128)(2,1)S(1)} %get-tuple-element.41), channel_id=1, source_target_pairs={{0,1},{1,0},{2,3},{3,2},{4,5},{5,4},{6,7},{7,6},{8,9},{9,8},{10,11... | collective-permute-start | bytes 2359304 | tf_op jit(solution)/shard_map/ppermute | solution.py:259
  163.8 29.3 %collective-permute-start.12 = (bf16[512,768]{1,0:T(8,128)(2,1)S(1)}, bf16[512,768]{1,0:T(8,128)(2,1)S(1)}, u32[]{:S(2)}, u32[]{:S(2)}) collective-permute-start(bf16[512,768]{1,0:T(8,128)(2,1)S(1)} %get-tuple-element.42), channel_id=1, source_target_pairs={{0,1},{1,0},{2,3},{3,2},{4,5},{5,4},{6,7},{7,6},{8,9},{9,8},{10,11... | collective-permute-start | bytes 2359304 | tf_op jit(solution)/shard_map/ppermute | solution.py:259
  (15 other events, 17.1 us)
Sparse Core Ops, SparseCore 0:
  9.1 77.1 all-gather.4
  108.0 39.6 all-gather.6
